TPU v7x, 512 devices: a whole 4x4x16 slice. The times are simulated.
512 devices in a mesh: tm: 16 (over z_lo, core), space: 32 (over y, x, z_hi).
Axes of the slice: x: 4, y: 4, z: 16 (z_hi: 2, z_lo: 8; z = z_hi * 8 + z_lo), core: 2. Of those that a mesh axis runs over, the one named last changes fastest.
Arguments:
- vectors: bfloat16 [16, 2, 32, 3, 256, 128], P('tm', None, 'space'), may hold values from -12 to 12
- gauge_links: float32 [16, 3, 2, 32, 3, 3, 128], P('tm', None, None, 'space'), may hold values from -2.5 to 2.5
- perambulator: bfloat16 [16, 256, 2, 256, 256], P('tm', 'space'), may hold values from -0.375 to 0.375
- directions: int32 [16], P('tm'), may hold values from 0 to 2
- momentum: int32 [3], replicated, may hold values from -2 to 2
- source_list: int32 [16], replicated, may hold values from 0 to 15, each once
Outputs:
- elementals: bfloat16 [16, 256, 2, 256], P('tm', 'space')
- correlator: float32 [2, 16, 16], P(None, 'tm')
Inputs may be any that keep to these rules, and one draw needn't show every extreme that they name: `directions`: 0, 1, 2 stand for x, y, z. `source_list`: each timeslice is the source of exactly one slot.
All inputs are finite; a program needn't handle non-finite values.
Results may differ from a plain program's by a relative error of at most 0.019.
Values may be sent and summed in bfloat16 or wider, within the bound.
No kernel may reach another device: no remote copies, remote signals or barrier semaphores. Data moves between devices by JAX's collectives and lax.ppermute only.
A program may use at most 64 MiB of HBM per device.

v0:
```python
import math

import jax
import jax.numpy as jnp
from jax import lax
from jax.sharding import PartitionSpec as P

NV = 256
NS = 4
SX = 16
SY = 8
SMEAR = 2


smear_kappa = 0.05


def shifted(block, axis, distance):
    devices = range(lax.axis_size(axis))
    route = [((i - distance) % len(devices), i) for i in devices]
    return lax.ppermute(block, axis, route)


def colour_apply(link_field, colour_field, adjoint):
    if adjoint:
        link_real = jnp.swapaxes(link_field[0], 1, 2)
        link_imag = -jnp.swapaxes(link_field[1], 1, 2)
    else:
        link_real = link_field[0]
        link_imag = link_field[1]

    def contract(matrix, vector):
        return jnp.sum(matrix[:, :, :, None, :] * vector[:, None, :, :, :], axis=2)

    out_real = contract(link_real, colour_field[0]) - contract(link_imag, colour_field[1])
    out_imag = contract(link_real, colour_field[1]) + contract(link_imag, colour_field[0])
    return jnp.stack([out_real, out_imag])


def ahead_x(colour_field):
    column = jnp.arange(colour_field.shape[-1]) % SX
    return jnp.where(
        column == SX - 1,
        jnp.roll(colour_field, SX - 1, axis=-1),
        jnp.roll(colour_field, -1, axis=-1),
    )


def behind_x(colour_field):
    column = jnp.arange(colour_field.shape[-1]) % SX
    return jnp.where(
        column == 0, jnp.roll(colour_field, 1 - SX, axis=-1), jnp.roll(colour_field, 1, axis=-1)
    )


def upper_plane(colour_field):
    arriving = shifted(colour_field, "space", -1)
    return jnp.concatenate([colour_field[:, 1:], arriving], axis=1)


def lower_plane(colour_field):
    arriving = shifted(colour_field, "space", 1)
    return jnp.concatenate([arriving, colour_field[:, :-1]], axis=1)


def smear_once(smeared, link_set):
    colour_field = smeared.astype(jnp.float32)
    summed = -6.0 * colour_field
    for direction in range(3):
        link_field = link_set[direction]
        if direction == 0:
            incoming = ahead_x(colour_field)
        elif direction == 1:
            incoming = jnp.roll(colour_field, -SX, axis=-1)
        else:
            incoming = upper_plane(smeared).astype(jnp.float32)
        carried = colour_apply(link_field, colour_field, True)
        if direction == 0:
            outgoing = behind_x(carried)
        elif direction == 1:
            outgoing = jnp.roll(carried, SX, axis=-1)
        else:
            outgoing = lower_plane(carried.astype(jnp.bfloat16)).astype(jnp.float32)
        summed = summed + colour_apply(link_field, incoming, False) + outgoing
    return (colour_field + smear_kappa * summed).astype(jnp.bfloat16)


def covariant_step(smeared, link_set, pick):
    colour_field = smeared.astype(jnp.float32)
    link_field = lax.dynamic_index_in_dim(link_set, pick, 0, keepdims=False)
    along_z = upper_plane(smeared).astype(jnp.float32)
    incoming = jnp.where(
        pick == 0,
        ahead_x(colour_field),
        jnp.where(pick == 1, jnp.roll(colour_field, -SX, axis=-1), along_z),
    )
    carried = colour_apply(link_field, colour_field, True)
    back_z = lower_plane(carried.astype(jnp.bfloat16)).astype(jnp.float32)
    outgoing = jnp.where(
        pick == 0, behind_x(carried), jnp.where(pick == 1, jnp.roll(carried, SX, axis=-1), back_z)
    )
    return colour_apply(link_field, incoming, False) - outgoing


def phase_angle(momentum, plane_index, extent):
    site_index = jnp.arange(SX * SY)
    column = (site_index % SX).astype(jnp.float32)
    row_index = (site_index // SX).astype(jnp.float32)
    moment = momentum.astype(jnp.float32)
    return (
        2.0
        * math.pi
        * (
            moment[0] * column[None, :] / SX
            + moment[1] * row_index[None, :] / SY
            + moment[2] * plane_index.astype(jnp.float32)[:, None] / extent
        )
    )


def project_half(gradient, angle_grid):
    cosine = jnp.cos(angle_grid)[:, None, None, :]
    sine_part = jnp.sin(angle_grid)[:, None, None, :]
    return jnp.stack(
        [
            cosine * gradient[0] + sine_part * gradient[1],
            cosine * gradient[1] - sine_part * gradient[0],
        ]
    ).astype(jnp.bfloat16)


def pair_up(projected):
    return jnp.stack([projected, jnp.stack([projected[1], -projected[0]])])


def per_device(vectors, gauge_links, perambulator, directions, momentum, source_list):
    smeared = vectors[0]
    link_set = gauge_links[0]
    block_set = perambulator[0]
    planes = smeared.shape[1]
    vector_count = smeared.shape[3]
    space_count = lax.axis_size("space")
    space_index = lax.axis_index("space")
    for sweep_index in range(SMEAR):
        smeared = smear_once(smeared, link_set)
    gradient = covariant_step(smeared, link_set, directions[0])
    plane_index = space_index * planes + jnp.arange(planes)
    angle_grid = phase_angle(momentum, plane_index, planes * space_count)
    projected = project_half(gradient, angle_grid)
    paired = pair_up(projected)
    scale_factor = 1.0 / math.sqrt(3 * SX * SY * planes * space_count)
    row_total = vector_count // space_count
    partial_value = jnp.einsum(
        "rzcas,orzcbs->aob", smeared, paired, preferred_element_type=jnp.float32
    )
    summed = lax.psum(partial_value, "space")
    elemental = (summed * scale_factor).astype(jnp.bfloat16)
    own_rows = lax.dynamic_slice_in_dim(elemental, space_index * row_total, row_total, 0)
    slot_index = space_index // (space_count // lax.axis_size("tm"))
    source = source_list[slot_index]
    gathered = lax.all_gather(elemental[None], "tm", axis=0, tiled=True)
    partner = lax.dynamic_index_in_dim(gathered, source, 0, keepdims=False)
    left_side = jnp.stack(
        [
            jnp.stack([elemental[:, 0], -elemental[:, 1]], 1),
            jnp.stack([elemental[:, 1], elemental[:, 0]], 1),
        ]
    )
    first = jnp.einsum(
        "pirk,brkj->pbij", left_side, block_set, preferred_element_type=jnp.float32
    ).astype(jnp.bfloat16)
    right_side = jnp.stack(
        [jnp.stack([partner[:, 0], partner[:, 1]]), jnp.stack([-partner[:, 1], partner[:, 0]])]
    )
    second = jnp.einsum("pbik,pqkj->qbij", first, right_side, preferred_element_type=jnp.float32)
    block_real = block_set[:, 0].astype(jnp.float32)
    block_imag = block_set[:, 1].astype(jnp.float32)
    trace_real = jnp.sum(second[0] * block_real + second[1] * block_imag)
    trace_imag = jnp.sum(second[1] * block_real - second[0] * block_imag)
    pair_value = jnp.stack([trace_real, trace_imag]) / (NS * NV)
    one_hot = (jnp.arange(source_list.shape[0]) == source).astype(jnp.float32)
    spread = pair_value[:, None] * one_hot[None, :]
    correlator = lax.psum(spread, "space")
    return (own_rows[None], correlator[:, None, :])


def solution(mesh):
    in_specs = (
        P("tm", None, "space", None, None, None),
        P("tm", None, None, "space", None, None, None),
        P("tm", "space", None, None, None),
        P("tm"),
        P(),
        P(),
    )
    out_specs = (P("tm", "space", None, None), P(None, "tm", None))
    return jax.shard_map(
        per_device, mesh=mesh, in_specs=in_specs, out_specs=out_specs, check_vma=False
    )
```

profile of v0, /device:TPU:2, one launch (start us, length us, event | category | flops | bytes accessed | tf_op | source)
XLA Modules:
  0.0 1123.3 jit_solution(13939225043957740746)
XLA Ops:
  10.3 2.0 multiply_reduce_fusion.35
  13.3 15.7 %collective-permute-start.1 = (bf16[2,1,3,256,128]{4,3,2,1,0:T(8,128)(2,1)}, bf16[2,1,3,256,128]{4,3,2,1,0:T(8,128)(2,1)}, u32[]{:S(2)}, u32[]{:S(2)}) collective-permute-start(bf16[2,1,3,256,128]{4,3,2,1,0:T(8,128)(2,1)} %pad_maximum_fusion.7), channel_id=1, source_target_pairs={{31,0},{0,1},{1,2},{2,3},{3,4},{4,5},{5,6},{6,7},{7,8},{8,9},{9,10... | collective-permute-start | bytes 1179656 | tf_op jit(solution)/shard_map/ppermute | solution.py:21
  29.0 1.9 collective-permute-start
  30.9 1.2 slice.423
  33.4 1.2 fusion.14
  43.0 1.2 multiply_reduce_fusion.55
  46.2 1.9 fusion.74
  50.7 5.1 collective-permute-done
  59.0 1.7 fusion.80
  60.7 33.1 %collective-permute-start.2 = (bf16[2,1,3,256,128]{4,3,2,1,0:T(8,128)(2,1)S(1)}, bf16[2,1,3,256,128]{4,3,2,1,0:T(8,128)(2,1)S(1)}, u32[]{:S(2)}, u32[]{:S(2)}) collective-permute-start(bf16[2,1,3,256,128]{4,3,2,1,0:T(8,128)(2,1)S(1)} %get-tuple-element.101), channel_id=1, source_target_pairs={{1,0},{2,1},{3,2},{4,3},{5,4},{6,5},{7,6},{8,7},{9,8},{10,9},{11,1... | collective-permute-start | bytes 1179656 | tf_op jit(solution)/shard_map/ppermute | solution.py:21
  97.0 23.2 %collective-permute-start.3 = (bf16[2,1,3,256,128]{4,3,2,1,0:T(8,128)(2,1)S(1)}, bf16[2,1,3,256,128]{4,3,2,1,0:T(8,128)(2,1)S(1)}, u32[]{:S(2)}, u32[]{:S(2)}) collective-permute-start(bf16[2,1,3,256,128]{4,3,2,1,0:T(8,128)(2,1)S(1)} %pad_maximum_fusion.8), channel_id=1, source_target_pairs={{31,0},{0,1},{1,2},{2,3},{3,4},{4,5},{5,6},{6,7},{7,8},{8,9},{9,10... | collective-permute-start | bytes 1179656 | tf_op jit(solution)/shard_map/ppermute | solution.py:21
  123.6 48.9 %collective-permute-done.2 = bf16[2,1,3,256,128]{4,3,2,1,0:T(8,128)(2,1)S(1)} collective-permute-done((bf16[2,1,3,256,128]{4,3,2,1,0:T(8,128)(2,1)S(1)}, bf16[2,1,3,256,128]{4,3,2,1,0:T(8,128)(2,1)S(1)}, u32[]{:S(2)}, u32[]{:S(2)}) %collective-permute-start.2) | collective-permute-done | bytes 393248 | tf_op jit(solution)/shard_map/ppermute | solution.py:21
  174.7 2.1 collective-permute-start.4
  177.7 18.9 %collective-permute-start.5 = (bf16[2,1,3,256,128]{4,3,2,1,0:T(8,128)(2,1)S(1)}, bf16[2,1,3,256,128]{4,3,2,1,0:T(8,128)(2,1)S(1)}, u32[]{:S(2)}, u32[]{:S(2)}) collective-permute-start(bf16[2,1,3,256,128]{4,3,2,1,0:T(8,128)(2,1)S(1)} %pad_maximum_fusion.9), channel_id=1, source_target_pairs={{31,0},{0,1},{1,2},{2,3},{3,4},{4,5},{5,6},{6,7},{7,8},{8,9},{9,10... | collective-permute-start | bytes 1179656 | tf_op jit(solution)/shard_map/ppermute | solution.py:21
  197.2 49.3 %collective-permute-done.4 = bf16[2,1,3,256,128]{4,3,2,1,0:T(8,128)(2,1)S(1)} collective-permute-done((bf16[2,1,3,256,128]{4,3,2,1,0:T(8,128)(2,1)S(1)}, bf16[2,1,3,256,128]{4,3,2,1,0:T(8,128)(2,1)S(1)}, u32[]{:S(2)}, u32[]{:S(2)}) %collective-permute-start.4) | collective-permute-done | bytes 393248 | tf_op jit(solution)/shard_map/ppermute | solution.py:21
  249.5 1.2 convolution_bitcast_fusion.1
  250.8 593.3 %all-reduce.2.cloned.1.call-done = f32[256,2,256]{2,0,1:T(8,128)} async-done(((f32[256,2,256]{2,0,1:T(8,128)}), f32[256,2,256]{2,0,1:T(8,128)}) %all-reduce.2.cloned.1.call-update) | async-done | bytes 524304 | tf_op jit(solution)/shard_map/psum | solution.py:156
  844.1 1.8 multiply_convert_fusion
  847.8 2.9 copy.54
  852.7 96.4 %all-gather.3.cloned.1.call-done = bf16[4096,2,256]{2,0,1:T(8,128)(2,1)} async-done(((bf16[256,2,256]{2,0,1:T(8,128)(2,1)}), bf16[4096,2,256]{2,0,1:T(8,128)(2,1)}) %all-gather.3.cloned.1.call-update) | async-done | bytes 4194320 | tf_op jit(solution)/shard_map/all_gather | solution.py:161
  950.3 5.9 convolution_bitcast_fusion
  956.2 3.5 fusion.1
  959.7 1.3 maximum_multiply_fusion
  961.1 155.3 %psum.15 = f32[2,1,16]{2,0,1:T(2,128)} all-reduce(f32[2,1,16]{2,0,1:T(2,128)S(1)} %multiply_bitcast_fusion), channel_id=1, replica_groups=mesh['tm'=16,'space'=32] {'space'}, use_global_device_ids=true, to_apply=%region_59.60 | all-reduce | flops 32 | bytes 256 | tf_op jit(solution)/shard_map/psum | solution.py:183
  (221 shorter events, 36.0 us)
Async XLA Ops:
  7.2 836.9 %all-reduce.2.cloned.1.call-start = ((), (), s32[]{:S(2)}) async-start(), calls=%async_computation | async-start | bytes 1048576 | tf_op jit(solution)/shard_map/psum | solution.py:156
  9.7 2.7 copy-start.10
  9.7 2.6 copy-start.12
  9.7 2.6 copy-start.14
  9.7 2.6 copy-start.16
  9.7 2.6 copy-start.18
  10.3 2.0 copy-start.20
  12.3 16.6 %copy-start.4 = (bf16[1,2,1,3,256,128]{5,4,3,2,1,0:T(8,128)(2,1)S(1)}, bf16[1,2,1,3,256,128]{5,4,3,2,1,0:T(8,128)(2,1)}, u32[]{:S(2)}) copy-start(bf16[1,2,1,3,256,128]{5,4,3,2,1,0:T(8,128)(2,1)} %param.6) | copy-start | bytes 1179652
  13.3 44.2 %collective-permute-start.1 = (bf16[2,1,3,256,128]{4,3,2,1,0:T(8,128)(2,1)}, bf16[2,1,3,256,128]{4,3,2,1,0:T(8,128)(2,1)}, u32[]{:S(2)}, u32[]{:S(2)}) collective-permute-start(bf16[2,1,3,256,128]{4,3,2,1,0:T(8,128)(2,1)} %pad_maximum_fusion.7), channel_id=1, source_target_pairs={{31,0},{0,1},{1,2},{2,3},{3,4},{4,5},{5,6},{6,7},{7,8},{8,9},{9,10... | collective-permute-start | bytes 1179656 | tf_op jit(solution)/shard_map/ppermute | solution.py:21
  29.0 26.8 %collective-permute-start = (bf16[2,1,3,256,128]{4,3,2,1,0:T(8,128)(2,1)S(1)}, bf16[2,1,3,256,128]{4,3,2,1,0:T(8,128)(2,1)}, u32[]{:S(2)}, u32[]{:S(2)}) collective-permute-start(bf16[2,1,3,256,128]{4,3,2,1,0:T(8,128)(2,1)S(1)} %bitcast.303), channel_id=1, source_target_pairs={{1,0},{2,1},{3,2},{4,3},{5,4},{6,5},{7,6},{8,7},{9,8},{10,9},{11,1... | collective-permute-start | bytes 1179656 | tf_op jit(solution)/shard_map/ppermute | solution.py:21
  36.1 1.6 copy-start.41
  37.8 2.3 copy-start.2
  41.4 1.6 copy-start.8
  41.4 1.6 copy-start.9
  60.7 111.9 %collective-permute-start.2 = (bf16[2,1,3,256,128]{4,3,2,1,0:T(8,128)(2,1)S(1)}, bf16[2,1,3,256,128]{4,3,2,1,0:T(8,128)(2,1)S(1)}, u32[]{:S(2)}, u32[]{:S(2)}) collective-permute-start(bf16[2,1,3,256,128]{4,3,2,1,0:T(8,128)(2,1)S(1)} %get-tuple-element.101), channel_id=1, source_target_pairs={{1,0},{2,1},{3,2},{4,3},{5,4},{6,5},{7,6},{8,7},{9,8},{10,9},{11,1... | collective-permute-start | bytes 1179656 | tf_op jit(solution)/shard_map/ppermute | solution.py:21
  96.8 23.4 %copy-start.46 = (pred[128]{0:T(512)(128)(4,1)S(1)}, pred[128]{0:T(512)(128)(4,1)}, u32[]{:S(2)}) copy-start(pred[128]{0:T(512)(128)(4,1)} %copy-done.45) | copy-start | bytes 388
  97.0 76.2 %collective-permute-start.3 = (bf16[2,1,3,256,128]{4,3,2,1,0:T(8,128)(2,1)S(1)}, bf16[2,1,3,256,128]{4,3,2,1,0:T(8,128)(2,1)S(1)}, u32[]{:S(2)}, u32[]{:S(2)}) collective-permute-start(bf16[2,1,3,256,128]{4,3,2,1,0:T(8,128)(2,1)S(1)} %pad_maximum_fusion.8), channel_id=1, source_target_pairs={{31,0},{0,1},{1,2},{2,3},{3,4},{4,5},{5,6},{6,7},{7,8},{8,9},{9,10... | collective-permute-start | bytes 1179656 | tf_op jit(solution)/shard_map/ppermute | solution.py:21
  174.7 2.1 copy-start.32
  174.7 2.1 copy-start.35
  174.7 71.8 %collective-permute-start.4 = (bf16[2,1,3,256,128]{4,3,2,1,0:T(8,128)(2,1)S(1)}, bf16[2,1,3,256,128]{4,3,2,1,0:T(8,128)(2,1)S(1)}, u32[]{:S(2)}, u32[]{:S(2)}) collective-permute-start(bf16[2,1,3,256,128]{4,3,2,1,0:T(8,128)(2,1)S(1)} %get-tuple-element.99), channel_id=1, source_target_pairs={{1,0},{2,1},{3,2},{4,3},{5,4},{6,5},{7,6},{8,7},{9,8},{10,9},{11,1... | collective-permute-start | bytes 1179656 | tf_op jit(solution)/shard_map/ppermute | solution.py:21
  177.7 70.7 %collective-permute-start.5 = (bf16[2,1,3,256,128]{4,3,2,1,0:T(8,128)(2,1)S(1)}, bf16[2,1,3,256,128]{4,3,2,1,0:T(8,128)(2,1)S(1)}, u32[]{:S(2)}, u32[]{:S(2)}) collective-permute-start(bf16[2,1,3,256,128]{4,3,2,1,0:T(8,128)(2,1)S(1)} %pad_maximum_fusion.9), channel_id=1, source_target_pairs={{31,0},{0,1},{1,2},{2,3},{3,4},{4,5},{5,6},{6,7},{7,8},{8,9},{9,10... | collective-permute-start | bytes 1179656 | tf_op jit(solution)/shard_map/ppermute | solution.py:21
  250.7 595.2 %copy-start.49 = (s32[16]{0:T(128)S(1)}, s32[16]{0:T(128)}, u32[]{:S(2)}) copy-start(s32[16]{0:T(128)} %param.11) | copy-start | bytes 196
  250.7 698.4 %all-gather.3.cloned.1.call-start = ((), (), s32[]{:S(2)}) async-start(), calls=%async_computation.1 | async-start | bytes 4456448 | tf_op jit(solution)/shard_map/all_gather | solution.py:161
  847.8 4.2 copy-start.3
  (34 other events, 32.2 us)
Sparse Core Ops, SparseCore 0:
  250.9 593.1 all-reduce.1
  846.2 102.9 all-gather.2
where the time goes:
time: 1120 us
  waiting for transfers between devices  793 us (71%)
  blocking collectives  155 us (14%)
  starting transfers between devices  94.9 us (8%)
  other arithmetic  37.4 us (3%)
  between operations  18.3 us (2%)
  local copies, waits for them, and re-layouts  17.1 us (2%)
    psum x1, waiting for transfers between devices, per_device(): summed = lax.psum(partial_value, 'space')  593 us
    psum x1, blocking collectives, per_device(): correlator = lax.psum(spread, 'space')  155 us
    ppermute x6, waiting for transfers between devices, shifted(): return lax.ppermute(block, axis, route)  103 us
    all_gather x1, waiting for transfers between devices, per_device(): gathered = lax.all_gather(elemental[None], 'tm', axis=0, tiled=True)  96.4 us
    ppermute x6, starting transfers between devices, shifted(): return lax.ppermute(block, axis, route)  94.8 us
  transfers between devices with their start and end apart: 8, of which 5 were waited for; matrix products, arithmetic and copies ran while one was open for 3% of the time, Pallas kernels for 0%

commit v1 on v0

v1 whole, which is shorter than its diff:
```python
import functools
import math

import jax
import jax.numpy as jnp
from jax import lax
from jax.experimental import pallas as pl
from jax.experimental.pallas import tpu as pltpu
from jax.sharding import Mesh, PartitionSpec as P

NV = 256
NS = 4
SX = 16
SY = 8
SITES = SX * SY
HALF = NV // 2
VROWS = 6 * HALF
LROWS = 64
KAPPA = 0.05

SPACE = ("y", "x", "zh")
XY = ("y", "x")
COLUMN = ("zl", "core", "zh")
CHUNK = 16


def whole():
    return pl.BlockSpec(memory_space=pltpu.VMEM)


def scalar():
    return pl.BlockSpec(memory_space=pltpu.SMEM)


def roll_lanes(value, shift):
    return pltpu.roll(value, shift % SITES, value.ndim - 1)


def ahead_x(value, last):
    return jnp.where(last, roll_lanes(value, SX - 1), roll_lanes(value, -1))


def behind_x(value, first):
    return jnp.where(first, roll_lanes(value, 1 - SX), roll_lanes(value, 1))


def smear_kernel(pick_ref, phase_ref, low_ref, mid_ref, high_ref, far_ref, left_ref, right_ref, link_ref, one_ref, two_ref):
    lane = lax.broadcasted_iota(jnp.int32, (18, SITES), 1) % SX
    for plane in range(6):
        source = (low_ref, mid_ref, high_ref)[plane // 2]
        block = source[plane % 2, pl.ds(VROWS, LROWS), :].astype(jnp.float32)
        link_ref[plane, pl.ds(0, LROWS), :] = block
        link_ref[plane, pl.ds(64, 18), :] = behind_x(block[0:18], lane == 0)
        link_ref[plane, pl.ds(88, 18), :] = roll_lanes(block[18:36], SX)

    def link(plane, base):
        return lambda part, row, column: link_ref[plane, pl.ds(base + part * 9 + row * 3 + column, 1), :]

    def apply(total, matrix, field, adjoint):
        for row in range(3):
            for column in range(3):
                if adjoint:
                    real, imag = matrix(0, column, row), matrix(1, column, row)
                    total[0][row] += real * field[0][column] + imag * field[1][column]
                    total[1][row] += real * field[1][column] - imag * field[0][column]
                else:
                    real, imag = matrix(0, row, column), matrix(1, row, column)
                    total[0][row] += real * field[0][column] - imag * field[1][column]
                    total[1][row] += real * field[1][column] + imag * field[0][column]

    column_of = lax.broadcasted_iota(jnp.int32, (CHUNK, SITES), 1) % SX
    last, first = column_of == SX - 1, column_of == 0
    pick = pick_ref[0]

    def each(field, change):
        return [[change(field[part][colour]) for colour in range(3)] for part in range(2)]

    def zeros():
        zero = jnp.zeros((CHUNK, SITES), jnp.float32)
        return [[zero for _ in range(3)] for _ in range(2)]

    def sweep(plane, here, above, below):
        total = zeros()
        apply(total, link(plane, 0), each(here, lambda v: ahead_x(v, last)), False)
        apply(total, link(plane, 64), each(here, lambda v: behind_x(v, first)), True)
        apply(total, link(plane, 18), each(here, lambda v: roll_lanes(v, -SX)), False)
        apply(total, link(plane, 88), each(here, lambda v: roll_lanes(v, SX)), True)
        apply(total, link(plane, 36), above, False)
        apply(total, link(plane - 1, 36), below, True)
        return [
            [
                here[part][colour] + KAPPA * (total[part][colour] - 6.0 * here[part][colour])
                for colour in range(3)
            ]
            for part in range(2)
        ]

    def rounded(value):
        return value.astype(jnp.bfloat16).astype(jnp.float32)

    def step(chunk, carry):
        start = pl.multiple_of(chunk * CHUNK, CHUNK)

        def start_field(plane):
            def get(part, colour):
                rows = pl.ds((part * 3 + colour) * HALF + start, CHUNK)
                if plane == 6:
                    return far_ref[rows, :].astype(jnp.float32)
                source = (low_ref, mid_ref, high_ref)[plane // 2]
                return source[plane % 2, rows, :].astype(jnp.float32)

            return [[get(part, colour) for colour in range(3)] for part in range(2)]

        def stored(ref, plane):
            return [[ref[plane, part * 3 + colour] for colour in range(3)] for part in range(2)]

        for plane in range(1, 6):
            result = sweep(plane, start_field(plane), start_field(plane + 1), start_field(plane - 1))
            for part in range(2):
                for colour in range(3):
                    one_ref[plane, part * 3 + colour] = rounded(result[part][colour])
        for plane in range(2, 5):
            result = sweep(plane, stored(one_ref, plane), stored(one_ref, plane + 1), stored(one_ref, plane - 1))
            for part in range(2):
                for colour in range(3):
                    two_ref[plane, part * 3 + colour] = rounded(result[part][colour])
        for side in range(2):
            plane = side + 2
            here, above = stored(two_ref, plane), stored(two_ref, plane + 1)
            incoming = [
                [
                    jnp.where(
                        pick == 0,
                        ahead_x(here[part][colour], last),
                        jnp.where(pick == 1, roll_lanes(here[part][colour], -SX), above[part][colour]),
                    )
                    for colour in range(3)
                ]
                for part in range(2)
            ]
            moved = zeros()
            apply(moved, link(plane, pick * 18), incoming, False)

            def row_of(index):
                return phase_ref[pl.ds(side * 4 + index, 1), :]

            for colour in range(3):

                def put(kind, part, left, real, imag):
                    index = ((kind * 2 + part) * 2 + side) * 3 + colour
                    lanes = pl.ds((index % 2) * SITES, SITES)
                    left_ref[index // 2, pl.ds(start, CHUNK), lanes] = left.astype(jnp.bfloat16)
                    right_ref[index // 2, pl.ds(start, CHUNK), lanes] = real.astype(jnp.bfloat16)
                    right_ref[index // 2, pl.ds(HALF + start, CHUNK), lanes] = imag.astype(jnp.bfloat16)

                def turned(field, base):
                    cosine, sine = row_of(base), row_of(base + 1)
                    return (
                        cosine * field[0][colour] - sine * field[1][colour],
                        cosine * field[1][colour] + sine * field[0][colour],
                    )

                real, imag = turned(moved, 0)
                put(0, 0, here[0][colour], real, imag)
                put(0, 1, here[1][colour], imag, -real)
                real, imag = turned(here, 2)
                put(1, 0, moved[0][colour], real, imag)
                put(1, 1, moved[1][colour], imag, -real)
        return carry

    lax.fori_loop(0, HALF // CHUNK, step, 0)


def smear(pick, phase, low, mid, high, far):
    return pl.pallas_call(
        smear_kernel,
        out_shape=(
            jax.ShapeDtypeStruct((12, HALF, 2 * SITES), jnp.bfloat16),
            jax.ShapeDtypeStruct((12, 2 * HALF, 2 * SITES), jnp.bfloat16),
        ),
        in_specs=[scalar(), whole(), whole(), whole(), whole(), whole()],
        out_specs=(whole(), whole()),
        scratch_shapes=[
            pltpu.VMEM((6, 112, SITES), jnp.float32),
            pltpu.VMEM((6, 6, CHUNK, SITES), jnp.float32),
            pltpu.VMEM((5, 6, CHUNK, SITES), jnp.float32),
        ],
        name="smear",
    )(pick, phase, low, mid, high, far)


def pair_kernel(core_ref, own_ref, other_ref, right_ref, out_ref):
    core = core_ref[0]

    def product(ref):
        total = jnp.zeros((HALF, 2 * HALF), jnp.float32)
        for index in range(12):
            total += lax.dot_general(
                ref[index], right_ref[index], (((1,), (1,)), ((), ())), preferred_element_type=jnp.float32
            )
        return total

    out_ref[pl.ds(pl.multiple_of(core * HALF, HALF), HALF), :] = product(own_ref)
    out_ref[pl.ds(pl.multiple_of((1 - core) * HALF, HALF), HALF), :] = product(other_ref)


def pair(core, own, other, right):
    return pl.pallas_call(
        pair_kernel,
        out_shape=jax.ShapeDtypeStruct((NV, 2 * HALF), jnp.float32),
        in_specs=[scalar(), whole(), whole(), whole()],
        out_specs=whole(),
        name="pair",
    )(core, own, other, right)


def spread_kernel(time_ref, source_ref, gathered_ref, out_ref):
    slots = out_ref.shape[0]

    def fetch(time):
        parts = [gathered_ref[(time // 2) * 4 + half * 2 + time % 2] for half in range(2)]
        return jnp.concatenate(
            [parts[half][:, part * HALF : (part + 1) * HALF] for part in range(2) for half in range(2)], axis=1
        )

    own = fetch(time_ref[0])
    for slot in range(slots):
        out_ref[slot, 0] = own
        out_ref[slot, 1] = fetch(source_ref[slot])


def spread(time, source_list, gathered):
    rows = gathered.shape[1]
    return pl.pallas_call(
        spread_kernel,
        out_shape=jax.ShapeDtypeStruct((source_list.shape[0], 2, rows, 2 * NV), jnp.bfloat16),
        in_specs=[scalar(), scalar(), whole()],
        out_specs=whole(),
        name="spread",
    )(time, source_list, gathered)


def trace_kernel(sink_ref, source_ref, block_ref, out_ref, left_ref):
    real, imag = sink_ref[:, :NV], sink_ref[:, NV:]
    left_ref[:NV, :NV] = real
    left_ref[:NV, NV:] = -imag
    left_ref[NV:, :NV] = imag
    left_ref[NV:, NV:] = real

    def folded(value):
        return jnp.sum(value.reshape(NV // 8, 8, NV), axis=0)

    def step(index, totals):
        block = block_ref[index]
        first = jnp.dot(left_ref[...], block, preferred_element_type=jnp.float32).astype(jnp.bfloat16)
        second = jnp.dot(first, source_ref[...], preferred_element_type=jnp.float32)
        second_real = second[:NV, :NV] - second[NV:, NV:]
        second_imag = second[:NV, NV:] + second[NV:, :NV]
        block_real = block[:NV].astype(jnp.float32)
        block_imag = block[NV:].astype(jnp.float32)
        return (
            totals[0] + folded(second_real * block_real + second_imag * block_imag),
            totals[1] + folded(second_imag * block_real - second_real * block_imag),
        )

    zero = jnp.zeros((8, NV), jnp.float32)
    totals = lax.fori_loop(0, block_ref.shape[0], step, (zero, zero))
    lane = lax.broadcasted_iota(jnp.int32, out_ref.shape, 1)
    out_ref[...] = jnp.where(lane == 0, jnp.sum(totals[0]), jnp.sum(totals[1]))


def trace(sink, source, blocks, copies):
    return pl.pallas_call(
        trace_kernel,
        out_shape=jax.ShapeDtypeStruct((copies, 128), jnp.float32),
        in_specs=[whole(), whole(), whole()],
        out_specs=whole(),
        scratch_shapes=[pltpu.VMEM((2 * NV, 2 * NV), jnp.bfloat16)],
        name="trace",
    )(sink, source, blocks)


def phases(momentum, pick, pair_index, extent):
    site = jnp.arange(SITES)
    column = (site % SX).astype(jnp.float32)
    row = (site // SX).astype(jnp.float32)
    moment = momentum.astype(jnp.float32)
    height = (pair_index * 2 + jnp.arange(2)).astype(jnp.float32)
    angle = (
        2.0
        * math.pi
        * (moment[0] * column[None] / SX + moment[1] * row[None] / SY + moment[2] * height[:, None] / extent)
    )
    step = jnp.where(pick == 0, moment[0] / SX, jnp.where(pick == 1, moment[1] / SY, moment[2] / extent))
    shifted = angle + 2.0 * math.pi * step
    return jnp.stack([jnp.cos(angle), -jnp.sin(angle), -jnp.cos(shifted), jnp.sin(shifted)], axis=1).reshape(8, SITES)


def per_device(vectors, gauge_links, perambulator, directions, momentum, source_list):
    core = lax.axis_index("core")
    level = lax.axis_index("zh")
    pair_index = lax.axis_index(XY)
    pairs = lax.axis_size(XY)
    rows = NV // pairs

    halves = vectors[0, :, 0].reshape(6, 2, HALF, SITES)
    link_rows = gauge_links[0, :, :, 0].reshape(54, SITES).astype(jnp.bfloat16)
    pick_row = jnp.broadcast_to(directions[0].astype(jnp.bfloat16), (LROWS - 54, SITES))
    tail = jnp.concatenate([link_rows, pick_row], axis=0)

    def half_of(index):
        half = lax.dynamic_index_in_dim(halves, index, 1, keepdims=False).reshape(VROWS, SITES)
        return jnp.concatenate([half, tail], axis=0)

    kept = half_of(level)
    given = half_of(1 - level)
    crossed = lax.ppermute(kept, ("core", "zh"), [(1, 2), (2, 1)])
    taken = lax.ppermute(given, ("core", "zh"), [(0, 2), (3, 1), (1, 0), (2, 3)])
    same = core == level
    own_plane = jnp.where(same, kept, taken)
    other_plane = jnp.where(same, taken, crossed)
    even = level == 0
    mid = jnp.stack([jnp.where(even, own_plane, other_plane), jnp.where(even, other_plane, own_plane)])

    def moved(value, distance):
        return lax.ppermute(value, XY, [(i, (i + distance) % pairs) for i in range(pairs)])

    high = moved(mid, -1)
    low = moved(mid, 1)
    far = moved(mid[0, :VROWS], -2)
    pick = mid[0, VROWS + 54, 0].astype(jnp.int32)
    phase = phases(momentum, pick, pair_index, 2 * pairs)
    left, right = smear(pick[None], phase, low, mid, high, far)
    other = lax.ppermute(left, "core", [(0, 1), (1, 0)])
    partial_value = pair(core[None], left, other, right)

    parts = lax.all_to_all(partial_value, XY, 0, 0, tiled=True).reshape(pairs, rows, 2 * HALF)
    scale = 1.0 / math.sqrt(3 * SITES * 2 * pairs)
    share = (jnp.sum(parts, axis=0) * scale).astype(jnp.bfloat16)

    column = lax.axis_size(COLUMN)
    copies = jnp.broadcast_to(share[None], (column, rows, 2 * HALF))
    gathered = lax.all_to_all(copies, COLUMN, 0, 0, tiled=True)
    time = lax.axis_index(("zl", "core"))
    sent = spread(time[None], source_list, gathered)
    arrived = lax.all_to_all(sent, XY, 0, 0, tiled=True)
    sink = arrived[:, 0].reshape(NV, 2 * NV)
    source = arrived[:, 1].reshape(NV, 2 * NV)

    space_count = lax.axis_size(SPACE)
    own_rows = NV // space_count
    elemental = lax.dynamic_slice_in_dim(sink, lax.axis_index(SPACE) * own_rows, own_rows, 0)
    blocks = perambulator[0].reshape(-1, 2 * NV, NV)
    value = trace(sink, source, blocks, space_count)
    values = lax.all_to_all(value, SPACE, 0, 0, tiled=True)[:, :2].reshape(pairs, 2, 2)
    per_slot = jnp.sum(values, axis=1) / (NS * NV)
    one_hot = (source_list[:, None] == jnp.arange(source_list.shape[0])[None]).astype(jnp.float32)
    correlator = jnp.sum(per_slot[:, :, None] * one_hot[:, None, :], axis=0)
    return elemental.reshape(1, own_rows, 2, NV), correlator[:, None, :]


def solution(mesh):
    grid = Mesh(mesh.devices.reshape(8, 2, 4, 4, 2), ("zl", "core", "y", "x", "zh"))
    times = ("zl", "core")
    in_specs = (
        P(times, None, SPACE, None, None, None),
        P(times, None, None, SPACE, None, None, None),
        P(times, SPACE, None, None, None),
        P(times),
        P(),
        P(),
    )
    out_specs = (P(times, SPACE, None, None), P(None, times, None))
    return jax.shard_map(per_device, mesh=grid, in_specs=in_specs, out_specs=out_specs, check_vma=False)
```

time: 1120 us -> 179 us (0.16)
  the two profiles are of different devices: /device:TPU:2 before, /device:TPU:32 now
where the time goes in v1:
time: 179 us; the launch traced here: 178 us
  waiting for transfers between devices  69.2 us (39%)
  starting transfers between devices  49.4 us (28%)
  Pallas kernels  27.7 us (15%)
  blocking collectives  14.8 us (8%)
  local copies, waits for them, and re-layouts  8.45 us (5%)
  other arithmetic  4.76 us (3%)
  between operations  4.1 us (2%)
    all_to_all x1, waiting for transfers between devices, per_device(): gathered = lax.all_to_all(copies, COLUMN, 0, 0, tiled=True)  20.7 us
    ppermute x1, waiting for transfers between devices, per_device(): lax.ppermute(given, ('core', 'zh'), [(0, 2), (3, 1), (1, 0), (2, 3)])  15.7 us
    all_to_all x1, waiting for transfers between devices, per_device(): lax.all_to_all(value, SPACE, 0, 0, tiled=True)[:, :2].reshape(pairs, 2, 2)  15.7 us
    all_to_all x1, blocking collectives, per_device(): lax.all_to_all(partial_value, XY, 0, 0, tiled=True)  14.8 us
    ppermute x1, starting transfers between devices, per_device(): other = lax.ppermute(left, 'core', [(0, 1), (1, 0)])  14.3 us
    pallas_call x1, Pallas kernels, smear(): pl.pallas_call(smear_kernel, out_shape=(jax.ShapeDtypeStruct((12, HALF, 2...  13.8 us
    ppermute x3, starting transfers between devices, moved(): lax.ppermute(value, XY, [(i, (i + distance) % pairs) for i in range(pairs)])  13.2 us
    all_to_all x1, waiting for transfers between devices, per_device(): arrived = lax.all_to_all(sent, XY, 0, 0, tiled=True)  11.5 us
  transfers between devices with their start and end apart: 9, of which 6 were waited for; matrix products, arithmetic and copies ran while one was open for 3% of the time, Pallas kernels for 0%

profile of v1, /device:TPU:32, one launch (start us, length us, event | category | flops | bytes accessed | tf_op | source)
XLA Modules:
  0.0 178.4 jit_solution(17737661735417745986)
XLA Ops:
  0.6 0.8 convert_reduce_fusion
  2.2 1.0 constant_dynamic-slice_fusion.2
  3.5 1.9 %collective-permute-start = (bf16[832,128]{1,0:T(8,128)(2,1)S(1)}, bf16[832,128]{1,0:T(8,128)(2,1)S(1)}, u32[]{:S(2)}, u32[]{:S(2)}) collective-permute-start(bf16[832,128]{1,0:T(8,128)(2,1)S(1)} %get-tuple-element.23), channel_id=1, source_target_pairs={{0,32},{33,1},{1,0},{32,33},{2,34},{35,3},{3,2},{34,35},{4,36},{37... | collective-permute-start | bytes 638984 | tf_op jit(solution)/shard_map/ppermute | solution.py:318
  9.3 1.3 fusion.9
  11.2 15.7 %collective-permute-done = bf16[832,128]{1,0:T(8,128)(2,1)S(1)} collective-permute-done((bf16[832,128]{1,0:T(8,128)(2,1)S(1)}, bf16[832,128]{1,0:T(8,128)(2,1)S(1)}, u32[]{:S(2)}, u32[]{:S(2)}) %collective-permute-start) | collective-permute-done | bytes 213024 | tf_op jit(solution)/shard_map/ppermute | solution.py:318
  27.2 3.4 %collective-permute-start.2 = (bf16[2,832,128]{2,1,0:T(8,128)(2,1)S(1)}, bf16[2,832,128]{2,1,0:T(8,128)(2,1)S(1)}, u32[]{:S(2)}, u32[]{:S(2)}) collective-permute-start(bf16[2,832,128]{2,1,0:T(8,128)(2,1)S(1)} %pad_maximum_fusion.mid_ref), channel_id=1, source_target_pairs={{0,2},{2,4},{4,6},{6,8},{8,10},{10,12},{12,14},{14,16},{16,18},{18... | collective-permute-start | bytes 1277960 | tf_op jit(solution)/shard_map/ppermute | solution.py:326
  30.6 5.8 %collective-permute-start.3 = (bf16[2,832,128]{2,1,0:T(8,128)(2,1)S(1)}, bf16[2,832,128]{2,1,0:T(8,128)(2,1)S(1)}, u32[]{:S(2)}, u32[]{:S(2)}) collective-permute-start(bf16[2,832,128]{2,1,0:T(8,128)(2,1)S(1)} %pad_maximum_fusion.mid_ref), channel_id=1, source_target_pairs={{0,30},{2,0},{4,2},{6,4},{8,6},{10,8},{12,10},{14,12},{16,14},{18,... | collective-permute-start | bytes 1277960 | tf_op jit(solution)/shard_map/ppermute | solution.py:326
  36.9 4.1 %collective-permute-start.4 = (bf16[768,128]{1,0:T(8,128)(2,1)S(1)}, bf16[768,128]{1,0:T(8,128)(2,1)S(1)}, u32[]{:S(2)}, u32[]{:S(2)}) collective-permute-start(bf16[768,128]{1,0:T(8,128)(2,1)S(1)} %slice_bitcast_fusion), channel_id=1, source_target_pairs={{0,28},{2,30},{4,0},{6,2},{8,4},{10,6},{12,8},{14,10},{16,12},{18,... | collective-permute-start | bytes 589832 | tf_op jit(solution)/shard_map/ppermute | solution.py:326
  42.4 3.6 %collective-permute-done.4.far_ref = bf16[768,128]{1,0:T(8,128)(2,1)S(1)} collective-permute-done((bf16[768,128]{1,0:T(8,128)(2,1)S(1)}, bf16[768,128]{1,0:T(8,128)(2,1)S(1)}, u32[]{:S(2)}, u32[]{:S(2)}) %collective-permute-start.4) | collective-permute-done | bytes 196640 | tf_op jit(solution)/shard_map/ppermute | solution.py:326
  47.0 13.8 %smear.1 = (bf16[12,128,256]{2,1,0:T(8,128)(2,1)}, bf16[12,256,256]{2,1,0:T(8,128)(2,1)}) custom-call(s32[1]{0:T(128)} %bitcast.7.pick_ref, f32[8,128]{1,0:T(8,128)} %bitcast.47, bf16[2,832,128]{2,1,0:T(8,128)(2,1)} %copy-done.3, bf16[2,832,128]{2,1,0:T(8,128)(2,1)} %copy-done, bf16[2,832,128]{2,1,0:T(8,128)(2,1)} %copy-done.4, bf16[768,128]{1,0:T(8,128)(2,1)} %copy-done.5), custom_call_target="tpu_custom_call" | custom-call | tf_op jit(solution)/shard_map/smear/pallas_call | solution.py:175
  60.8 14.3 %collective-permute-start.5 = (bf16[12,128,256]{2,1,0:T(8,128)(2,1)}, bf16[12,128,256]{2,1,0:T(8,128)(2,1)S(1)}, u32[]{:S(2)}, u32[]{:S(2)}) collective-permute-start(bf16[12,128,256]{2,1,0:T(8,128)(2,1)} %get-tuple-element.4.own_ref), channel_id=1, source_target_pairs={{0,32},{32,0},{1,33},{33,1},{2,34},{34,2},{3,35},{35,3},{4,36},{36... | collective-permute-start | bytes 2359304 | tf_op jit(solution)/shard_map/ppermute | solution.py:334
  75.1 2.1 %collective-permute-done.5.other_ref = bf16[12,128,256]{2,1,0:T(8,128)(2,1)S(1)} collective-permute-done((bf16[12,128,256]{2,1,0:T(8,128)(2,1)}, bf16[12,128,256]{2,1,0:T(8,128)(2,1)S(1)}, u32[]{:S(2)}, u32[]{:S(2)}) %collective-permute-start.5) | collective-permute-done | bytes 786464 | tf_op jit(solution)/shard_map/ppermute | solution.py:334
  77.2 0.9 copy-done.2
  78.1 3.7 %pair.1 = f32[256,256]{1,0:T(8,128)} custom-call(s32[1]{0:T(128)} %bitcast.1.core_ref, bf16[12,128,256]{2,1,0:T(8,128)(2,1)} %get-tuple-element.4.own_ref, bf16[12,128,256]{2,1,0:T(8,128)(2,1)} %copy-done.2, bf16[12,256,256]{2,1,0:T(8,128)(2,1)} %get-tuple-element.5.right_ref), custom_call_target="tpu_custom_call" | custom-call | tf_op jit(solution)/shard_map/pair/pallas_call | solution.py:208
  81.8 14.8 %all_to_all.31 = f32[16,16,256]{2,1,0:T(8,128)S(1)} all-to-all(f32[16,16,256]{2,1,0:T(8,128)} %bitcast.41), channel_id=1, replica_groups=mesh['zl'=8,'core'=2,'y'=4,'x'=4,'zh'=2] {'y','x'}, dimensions={0} | all-to-all | bytes 524288 | tf_op jit(solution)/shard_map/all_to_all | solution.py:337
  97.4 10.5 %all-to-all-start.1 = ((bf16[32,16,256]{2,1,0:T(8,128)(2,1)}), bf16[32,16,256]{2,1,0:T(8,128)(2,1)S(1)}, u32[]{:S(2)}, u32[]{:S(2)}) async-start(bf16[32,16,256]{2,1,0:T(8,128)(2,1)} %broadcast_in_dim.32), calls=%async_computation.1 | async-start | bytes 524288 | tf_op jit(solution)/shard_map/all_to_all | solution.py:343
  107.9 20.7 %all-to-all-done.1.gathered_ref = bf16[32,16,256]{2,1,0:T(8,128)(2,1)S(1)} async-done(((bf16[32,16,256]{2,1,0:T(8,128)(2,1)}), bf16[32,16,256]{2,1,0:T(8,128)(2,1)S(1)}, u32[]{:S(2)}, u32[]{:S(2)}) %all-to-all-start.1) | async-done | bytes 262176 | tf_op jit(solution)/shard_map/all_to_all | solution.py:343
  129.3 1.9 %spread.1 = bf16[16,2,16,512]{3,2,1,0:T(8,128)(2,1)} custom-call(s32[1]{0:T(128)} %bitcast.time_ref, s32[16]{0:T(128)} %source_ref.1, bf16[32,16,256]{2,1,0:T(8,128)(2,1)} %copy-done.1), custom_call_target="tpu_custom_call" | custom-call | tf_op jit(solution)/shard_map/spread/pallas_call | solution.py:234
  131.2 3.6 %all-to-all-start.2 = ((bf16[16,2,16,512]{3,2,1,0:T(8,128)(2,1)}), bf16[16,2,16,512]{3,2,1,0:T(8,128)(2,1)S(1)}, u32[]{:S(2)}, u32[]{:S(2)}) async-start(bf16[16,2,16,512]{3,2,1,0:T(8,128)(2,1)} %spread.1), calls=%async_computation.2 | async-start | bytes 1048576 | tf_op jit(solution)/shard_map/all_to_all | solution.py:346
  134.9 11.5 %all-to-all-done.2 = bf16[16,2,16,512]{3,2,1,0:T(8,128)(2,1)S(1)} async-done(((bf16[16,2,16,512]{3,2,1,0:T(8,128)(2,1)}), bf16[16,2,16,512]{3,2,1,0:T(8,128)(2,1)S(1)}, u32[]{:S(2)}, u32[]{:S(2)}) %all-to-all-start.2) | async-done | bytes 524320 | tf_op jit(solution)/shard_map/all_to_all | solution.py:346
  146.3 0.8 fusion.13
  147.1 8.3 %trace.1 = f32[32,128]{1,0:T(8,128)} custom-call(bf16[256,512]{1,0:T(8,128)(2,1)} %bitcast.39, bf16[256,512]{1,0:T(8,128)(2,1)} %bitcast.42, bf16[8,512,256]{2,1,0:T(8,128)(2,1)} %bitcast.36), custom_call_target="tpu_custom_call" | custom-call | tf_op jit(solution)/shard_map/trace/pallas_call | solution.py:273
  155.4 5.3 %all-to-all-start.3 = ((f32[32,1,128]{2,1,0:T(1,128)}), f32[32,1,128]{2,1,0:T(1,128)S(1)}, u32[]{:S(2)}, u32[]{:S(2)}) async-start(f32[32,1,128]{2,1,0:T(1,128)} %bitcast.45), calls=%async_computation.3 | async-start | bytes 32768 | tf_op jit(solution)/shard_map/all_to_all | solution.py:355
  162.0 15.7 %all-to-all-done.3 = f32[32,1,128]{2,1,0:T(1,128)S(1)} async-done(((f32[32,1,128]{2,1,0:T(1,128)}), f32[32,1,128]{2,1,0:T(1,128)S(1)}, u32[]{:S(2)}, u32[]{:S(2)}) %all-to-all-start.3) | async-done | bytes 16416 | tf_op jit(solution)/shard_map/all_to_all | solution.py:355
  (41 shorter events, 9.0 us)
Async XLA Ops:
  3.5 23.4 %collective-permute-start = (bf16[832,128]{1,0:T(8,128)(2,1)S(1)}, bf16[832,128]{1,0:T(8,128)(2,1)S(1)}, u32[]{:S(2)}, u32[]{:S(2)}) collective-permute-start(bf16[832,128]{1,0:T(8,128)(2,1)S(1)} %get-tuple-element.23), channel_id=1, source_target_pairs={{0,32},{33,1},{1,0},{32,33},{2,34},{35,3},{3,2},{34,35},{4,36},{37... | collective-permute-start | bytes 638984 | tf_op jit(solution)/shard_map/ppermute | solution.py:318
  5.4 21.5 %collective-permute-start.1 = (bf16[832,128]{1,0:T(8,128)(2,1)S(1)}, bf16[832,128]{1,0:T(8,128)(2,1)S(1)}, u32[]{:S(2)}, u32[]{:S(2)}) collective-permute-start(bf16[832,128]{1,0:T(8,128)(2,1)S(1)} %get-tuple-element.22), channel_id=1, source_target_pairs={{1,32},{32,1},{3,34},{34,3},{5,36},{36,5},{7,38},{38,7},{9,40},{40... | collective-permute-start | bytes 638984 | tf_op jit(solution)/shard_map/ppermute | solution.py:317
  27.2 18.8 %copy-start = (bf16[2,832,128]{2,1,0:T(8,128)(2,1)}, bf16[2,832,128]{2,1,0:T(8,128)(2,1)S(1)}, u32[]{:S(2)}) copy-start(bf16[2,832,128]{2,1,0:T(8,128)(2,1)S(1)} %pad_maximum_fusion.mid_ref) | copy-start | bytes 1277956
  27.2 18.8 %collective-permute-start.2 = (bf16[2,832,128]{2,1,0:T(8,128)(2,1)S(1)}, bf16[2,832,128]{2,1,0:T(8,128)(2,1)S(1)}, u32[]{:S(2)}, u32[]{:S(2)}) collective-permute-start(bf16[2,832,128]{2,1,0:T(8,128)(2,1)S(1)} %pad_maximum_fusion.mid_ref), channel_id=1, source_target_pairs={{0,2},{2,4},{4,6},{6,8},{8,10},{10,12},{12,14},{14,16},{16,18},{18... | collective-permute-start | bytes 1277960 | tf_op jit(solution)/shard_map/ppermute | solution.py:326
  30.6 15.4 %collective-permute-start.3 = (bf16[2,832,128]{2,1,0:T(8,128)(2,1)S(1)}, bf16[2,832,128]{2,1,0:T(8,128)(2,1)S(1)}, u32[]{:S(2)}, u32[]{:S(2)}) collective-permute-start(bf16[2,832,128]{2,1,0:T(8,128)(2,1)S(1)} %pad_maximum_fusion.mid_ref), channel_id=1, source_target_pairs={{0,30},{2,0},{4,2},{6,4},{8,6},{10,8},{12,10},{14,12},{16,14},{18,... | collective-permute-start | bytes 1277960 | tf_op jit(solution)/shard_map/ppermute | solution.py:326
  36.9 9.1 %collective-permute-start.4 = (bf16[768,128]{1,0:T(8,128)(2,1)S(1)}, bf16[768,128]{1,0:T(8,128)(2,1)S(1)}, u32[]{:S(2)}, u32[]{:S(2)}) collective-permute-start(bf16[768,128]{1,0:T(8,128)(2,1)S(1)} %slice_bitcast_fusion), channel_id=1, source_target_pairs={{0,28},{2,30},{4,0},{6,2},{8,4},{10,6},{12,8},{14,10},{16,12},{18,... | collective-permute-start | bytes 589832 | tf_op jit(solution)/shard_map/ppermute | solution.py:326
  46.0 0.7 copy-start.5
  46.0 0.8 copy-start.3
  46.0 1.0 copy-start.4
  60.8 16.4 %collective-permute-start.5 = (bf16[12,128,256]{2,1,0:T(8,128)(2,1)}, bf16[12,128,256]{2,1,0:T(8,128)(2,1)S(1)}, u32[]{:S(2)}, u32[]{:S(2)}) collective-permute-start(bf16[12,128,256]{2,1,0:T(8,128)(2,1)} %get-tuple-element.4.own_ref), channel_id=1, source_target_pairs={{0,32},{32,0},{1,33},{33,1},{2,34},{34,2},{3,35},{35,3},{4,36},{36... | collective-permute-start | bytes 2359304 | tf_op jit(solution)/shard_map/ppermute | solution.py:334
  77.2 0.9 copy-start.2
  81.8 53.0 %copy-start.6 = (s32[16]{0:T(128)S(1)}, s32[16]{0:T(128)}, u32[]{:S(2)}) copy-start(s32[16]{0:T(128)} %source_ref.1) | copy-start | bytes 196
  97.4 31.2 %all-to-all-start.1 = ((bf16[32,16,256]{2,1,0:T(8,128)(2,1)}), bf16[32,16,256]{2,1,0:T(8,128)(2,1)S(1)}, u32[]{:S(2)}, u32[]{:S(2)}) async-start(bf16[32,16,256]{2,1,0:T(8,128)(2,1)} %broadcast_in_dim.32), calls=%async_computation.1 | async-start | bytes 524288 | tf_op jit(solution)/shard_map/all_to_all | solution.py:343
  128.6 0.7 copy-start.1
  131.2 15.1 %all-to-all-start.2 = ((bf16[16,2,16,512]{3,2,1,0:T(8,128)(2,1)}), bf16[16,2,16,512]{3,2,1,0:T(8,128)(2,1)S(1)}, u32[]{:S(2)}, u32[]{:S(2)}) async-start(bf16[16,2,16,512]{3,2,1,0:T(8,128)(2,1)} %spread.1), calls=%async_computation.2 | async-start | bytes 1048576 | tf_op jit(solution)/shard_map/all_to_all | solution.py:346
  155.4 22.3 %all-to-all-start.3 = ((f32[32,1,128]{2,1,0:T(1,128)}), f32[32,1,128]{2,1,0:T(1,128)S(1)}, u32[]{:S(2)}, u32[]{:S(2)}) async-start(f32[32,1,128]{2,1,0:T(1,128)} %bitcast.45), calls=%async_computation.3 | async-start | bytes 32768 | tf_op jit(solution)/shard_map/all_to_all | solution.py:355

commit v2 on v1

v2 whole, which is shorter than its diff:
```python
import math

import jax
import jax.numpy as jnp
from jax import lax
from jax.experimental import pallas as pl
from jax.experimental.pallas import tpu as pltpu
from jax.sharding import Mesh, PartitionSpec as P

NV = 256
NS = 4
SX = 16
SY = 8
SITES = SX * SY
HALF = NV // 2
VROWS = 6 * HALF
LROWS = 64
KAPPA = 0.05

SPACE = ("y", "x", "zh")
XY = ("y", "x")
CHUNK = 16


def whole():
    return pl.BlockSpec(memory_space=pltpu.VMEM)


def scalar():
    return pl.BlockSpec(memory_space=pltpu.SMEM)


def roll_lanes(value, shift):
    return pltpu.roll(value, shift % SITES, value.ndim - 1)


def ahead_x(value, last):
    return jnp.where(last, roll_lanes(value, SX - 1), roll_lanes(value, -1))


def behind_x(value, first):
    return jnp.where(first, roll_lanes(value, 1 - SX), roll_lanes(value, 1))


def smear_kernel(pick_ref, phase_ref, low_ref, mid_ref, high_ref, far_ref, left_ref, right_ref, link_ref, one_ref, two_ref):
    site = lax.broadcasted_iota(jnp.int32, (18, SITES), 1) % SX
    for plane in range(6):
        source = (low_ref, mid_ref, high_ref)[plane // 2]
        block = source[plane % 2, pl.ds(VROWS, LROWS), :].astype(jnp.float32)
        rows = [block[index : index + 1] for index in range(54)]
        if plane:
            behind = behind_x(block[0:18], site == 0)
            below = roll_lanes(block[18:36], SX)
            rows += [behind[index : index + 1] for index in range(18)]
            rows += [below[index : index + 1] for index in range(18)]
        for index in range(36 if plane == 0 else 0, len(rows)):
            link_ref[plane, index] = jnp.broadcast_to(rows[index], (CHUNK, SITES)).astype(jnp.bfloat16)

    def link(plane, base):
        return lambda part, row, column: link_ref[plane, base + part * 9 + row * 3 + column]

    def apply(total, matrix, field, adjoint):
        for row in range(3):
            for column in range(3):
                if adjoint:
                    real, imag = matrix(0, column, row), matrix(1, column, row)
                    total[0][row] += real * field[0][column] + imag * field[1][column]
                    total[1][row] += real * field[1][column] - imag * field[0][column]
                else:
                    real, imag = matrix(0, row, column), matrix(1, row, column)
                    total[0][row] += real * field[0][column] - imag * field[1][column]
                    total[1][row] += real * field[1][column] + imag * field[0][column]

    column_of = lax.broadcasted_iota(jnp.int32, (CHUNK, SITES), 1) % SX
    last, first = column_of == SX - 1, column_of == 0
    pick = pick_ref[0]

    def each(field, change):
        return [[change(field[part][colour]) for colour in range(3)] for part in range(2)]

    def zeros(kind):
        zero = jnp.zeros((CHUNK, SITES), kind)
        return [[zero for _ in range(3)] for _ in range(2)]

    def sweep(plane, here, above, below):
        total = zeros(jnp.bfloat16)
        apply(total, link(plane, 0), each(here, lambda v: ahead_x(v, last)), False)
        apply(total, link(plane, 54), each(here, lambda v: behind_x(v, first)), True)
        apply(total, link(plane, 18), each(here, lambda v: roll_lanes(v, -SX)), False)
        apply(total, link(plane, 72), each(here, lambda v: roll_lanes(v, SX)), True)
        apply(total, link(plane, 36), above, False)
        apply(total, link(plane - 1, 36), below, True)

        def joined(part, colour):
            middle = here[part][colour].astype(jnp.float32)
            change = total[part][colour].astype(jnp.float32) - 6.0 * middle
            return (middle + KAPPA * change).astype(jnp.bfloat16)

        return [[joined(part, colour) for colour in range(3)] for part in range(2)]

    def step(chunk, carry):
        start = pl.multiple_of(chunk * CHUNK, CHUNK)

        def start_field(plane):
            def get(part, colour):
                rows = pl.ds((part * 3 + colour) * HALF + start, CHUNK)
                if plane == 6:
                    return far_ref[rows, :]
                source = (low_ref, mid_ref, high_ref)[plane // 2]
                return source[plane % 2, rows, :]

            return [[get(part, colour) for colour in range(3)] for part in range(2)]

        def stored(ref, plane):
            return [[ref[plane, part * 3 + colour] for colour in range(3)] for part in range(2)]

        for plane in range(1, 6):
            result = sweep(plane, start_field(plane), start_field(plane + 1), start_field(plane - 1))
            for part in range(2):
                for colour in range(3):
                    one_ref[plane, part * 3 + colour] = result[part][colour]
        for plane in range(2, 5):
            result = sweep(plane, stored(one_ref, plane), stored(one_ref, plane + 1), stored(one_ref, plane - 1))
            for part in range(2):
                for colour in range(3):
                    two_ref[plane, part * 3 + colour] = result[part][colour]
        for side in range(2):
            plane = side + 2
            here = each(stored(two_ref, plane), lambda v: v.astype(jnp.float32))
            above = each(stored(two_ref, plane + 1), lambda v: v.astype(jnp.float32))
            incoming = [
                [
                    jnp.where(
                        pick == 0,
                        ahead_x(here[part][colour], last),
                        jnp.where(pick == 1, roll_lanes(here[part][colour], -SX), above[part][colour]),
                    )
                    for colour in range(3)
                ]
                for part in range(2)
            ]
            moved = zeros(jnp.float32)
            chosen = link(plane, pick * 18)
            apply(moved, lambda *at: chosen(*at).astype(jnp.float32), incoming, False)

            def row_of(index):
                return phase_ref[pl.ds(side * 4 + index, 1), :]

            for colour in range(3):

                def put(kind, part, left, real, imag):
                    index = ((kind * 2 + part) * 2 + side) * 3 + colour
                    lanes = pl.ds((index % 2) * SITES, SITES)
                    left_ref[index // 2, pl.ds(start, CHUNK), lanes] = left.astype(jnp.bfloat16)
                    right_ref[index // 2, pl.ds(start, CHUNK), lanes] = real.astype(jnp.bfloat16)
                    right_ref[index // 2, pl.ds(HALF + start, CHUNK), lanes] = imag.astype(jnp.bfloat16)

                def turned(field, base):
                    cosine, sine = row_of(base), row_of(base + 1)
                    return (
                        cosine * field[0][colour] - sine * field[1][colour],
                        cosine * field[1][colour] + sine * field[0][colour],
                    )

                real, imag = turned(moved, 0)
                put(0, 0, here[0][colour], real, imag)
                put(0, 1, here[1][colour], imag, -real)
                real, imag = turned(here, 2)
                put(1, 0, moved[0][colour], real, imag)
                put(1, 1, moved[1][colour], imag, -real)
        return carry

    lax.fori_loop(0, HALF // CHUNK, step, 0)


def smear(pick, phase, low, mid, high, far):
    return pl.pallas_call(
        smear_kernel,
        out_shape=(
            jax.ShapeDtypeStruct((12, HALF, 2 * SITES), jnp.bfloat16),
            jax.ShapeDtypeStruct((12, 2 * HALF, 2 * SITES), jnp.bfloat16),
        ),
        in_specs=[scalar(), whole(), whole(), whole(), whole(), whole()],
        out_specs=(whole(), whole()),
        scratch_shapes=[
            pltpu.VMEM((6, 90, CHUNK, SITES), jnp.bfloat16),
            pltpu.VMEM((6, 6, CHUNK, SITES), jnp.bfloat16),
            pltpu.VMEM((5, 6, CHUNK, SITES), jnp.bfloat16),
        ],
        name="smear",
    )(pick, phase, low, mid, high, far)


def product(left_ref, right_ref):
    total = jnp.zeros((HALF, 2 * HALF), jnp.float32)
    for index in range(12):
        total += lax.dot_general(
            left_ref[index], right_ref[index], (((1,), (1,)), ((), ())), preferred_element_type=jnp.float32
        )
    return total.astype(jnp.bfloat16)


def own_kernel(left_ref, right_ref, out_ref):
    out_ref[...] = product(left_ref, right_ref)


def own_pair(left, right):
    return pl.pallas_call(
        own_kernel,
        out_shape=jax.ShapeDtypeStruct((HALF, 2 * HALF), jnp.bfloat16),
        in_specs=[whole(), whole()],
        out_specs=whole(),
        cost_estimate=pl.CostEstimate(flops=2 * 12 * HALF * 2 * HALF * 2 * SITES, bytes_accessed=3 * 2**20, transcendentals=0),
        name="own_pair",
    )(left, right)


def both_kernel(core_ref, own_ref, left_ref, right_ref, out_ref):
    core = core_ref[0]
    out_ref[pl.ds(pl.multiple_of(core * HALF, HALF), HALF), :] = own_ref[...]
    out_ref[pl.ds(pl.multiple_of((1 - core) * HALF, HALF), HALF), :] = product(left_ref, right_ref)


def both_pair(core, own, left, right):
    return pl.pallas_call(
        both_kernel,
        out_shape=jax.ShapeDtypeStruct((NV, 2 * HALF), jnp.bfloat16),
        in_specs=[scalar(), whole(), whole(), whole()],
        out_specs=whole(),
        name="both_pair",
    )(core, own, left, right)


def spread_kernel(level_ref, source_ref, gathered_ref, out_ref):
    slots = source_ref.shape[0]
    for core in range(2):
        own = gathered_ref[level_ref[0] * 2 + core]
        for slot in range(slots):
            out_ref[core * slots + slot, 0] = own
            out_ref[core * slots + slot, 1] = gathered_ref[source_ref[slot]]


def spread(level, source_list, gathered):
    rows = gathered.shape[1]
    return pl.pallas_call(
        spread_kernel,
        out_shape=jax.ShapeDtypeStruct((2 * source_list.shape[0], 2, rows, 2 * HALF), jnp.bfloat16),
        in_specs=[scalar(), scalar(), whole()],
        out_specs=whole(),
        name="spread",
    )(level, source_list, gathered)


def trace_kernel(arrived_ref, block_ref, out_ref, left_ref, source_ref):
    shares, rows = arrived_ref.shape[0] // 2, arrived_ref.shape[2]
    for share in range(shares):
        at = pl.ds(share * rows, rows)
        below = pl.ds(NV + share * rows, rows)
        for half in range(2):
            for part in range(2):
                lanes = pl.ds(part * NV + half * HALF, HALF)
                source_ref[at, lanes] = arrived_ref[half * shares + share, 1, :, pl.ds(part * HALF, HALF)]
            real = arrived_ref[half * shares + share, 0, :, pl.ds(0, HALF)]
            imag = arrived_ref[half * shares + share, 0, :, pl.ds(HALF, HALF)]
            here, there = pl.ds(half * HALF, HALF), pl.ds(NV + half * HALF, HALF)
            left_ref[at, here] = real
            left_ref[at, there] = -imag
            left_ref[below, here] = imag
            left_ref[below, there] = real

    def folded(value):
        return jnp.sum(value.reshape(NV // 8, 8, NV), axis=0)

    totals = [jnp.zeros((8, NV), jnp.float32)] * 2
    for index in range(block_ref.shape[0]):
        block = block_ref[index]
        first = jnp.dot(left_ref[...], block, preferred_element_type=jnp.float32).astype(jnp.bfloat16)
        second = jnp.dot(first, source_ref[...], preferred_element_type=jnp.float32)
        second_real = second[:NV, :NV] - second[NV:, NV:]
        second_imag = second[:NV, NV:] + second[NV:, :NV]
        block_real = block[:NV].astype(jnp.float32)
        block_imag = block[NV:].astype(jnp.float32)
        totals = [
            totals[0] + folded(second_real * block_real + second_imag * block_imag),
            totals[1] + folded(second_imag * block_real - second_real * block_imag),
        ]
    lane = lax.broadcasted_iota(jnp.int32, out_ref.shape, 1)
    out_ref[...] = jnp.where(lane == 0, jnp.sum(totals[0]), jnp.sum(totals[1]))


def trace(arrived, blocks, copies):
    return pl.pallas_call(
        trace_kernel,
        out_shape=jax.ShapeDtypeStruct((copies, 128), jnp.float32),
        in_specs=[whole(), whole()],
        out_specs=whole(),
        scratch_shapes=[pltpu.VMEM((2 * NV, 2 * NV), jnp.bfloat16), pltpu.VMEM((NV, 2 * NV), jnp.bfloat16)],
        name="trace",
    )(arrived, blocks)


def phases(momentum, pick, pair_index, extent):
    site = jnp.arange(SITES)
    column = (site % SX).astype(jnp.float32)
    row = (site // SX).astype(jnp.float32)
    moment = momentum.astype(jnp.float32)
    height = (pair_index * 2 + jnp.arange(2)).astype(jnp.float32)
    angle = (
        2.0
        * math.pi
        * (moment[0] * column[None] / SX + moment[1] * row[None] / SY + moment[2] * height[:, None] / extent)
    )
    step = jnp.where(pick == 0, moment[0] / SX, jnp.where(pick == 1, moment[1] / SY, moment[2] / extent))
    shifted = angle + 2.0 * math.pi * step
    return jnp.stack([jnp.cos(angle), -jnp.sin(angle), -jnp.cos(shifted), jnp.sin(shifted)], axis=1).reshape(8, SITES)


def per_device(vectors, gauge_links, perambulator, directions, momentum, source_list):
    core = lax.axis_index("core")
    level = lax.axis_index("zh")
    pair_index = lax.axis_index(XY)
    pairs = lax.axis_size(XY)
    rows = NV // pairs

    halves = jnp.swapaxes(vectors[0, :, 0].reshape(6, 2, HALF, SITES), 0, 1).reshape(2, VROWS, SITES)
    link_rows = gauge_links[0, :, :, 0].reshape(54, SITES).astype(jnp.bfloat16)
    pick_row = jnp.broadcast_to(directions[0].astype(jnp.bfloat16), (LROWS - 54, SITES))
    tail = jnp.concatenate([link_rows, pick_row], axis=0)
    plane = jnp.concatenate([halves, jnp.broadcast_to(tail[None], (2, LROWS, SITES))], axis=1)
    crossed = lax.ppermute(plane, ("core", "zh"), [(1, 0), (2, 3)])
    even = level == 0

    def both_planes(index):
        near = lax.dynamic_index_in_dim(plane, index, 0, keepdims=False)
        away = lax.dynamic_index_in_dim(crossed, index, 0, keepdims=False)
        return jnp.stack([jnp.where(even, near, away), jnp.where(even, away, near)])

    taken = lax.ppermute(both_planes(1 - core), ("core", "zh"), [(0, 2), (3, 1)])
    mid = jnp.where(core == level, both_planes(core), taken)

    def moved(value, distance):
        return lax.ppermute(value, XY, [(i, (i + distance) % pairs) for i in range(pairs)])

    high = moved(mid, -1)
    low = moved(mid, 1)
    far = moved(mid[0, :VROWS], -2)
    pick = mid[0, VROWS + 54, 0].astype(jnp.int32)
    phase = phases(momentum, pick, pair_index, 2 * pairs)
    left, right = smear(pick[None], phase, low, mid, high, far)
    other = lax.ppermute(left, "core", [(0, 1), (1, 0)])
    partial_value = both_pair(core[None], own_pair(left, right), other, right)

    parts = lax.all_to_all(partial_value, XY, 0, 0, tiled=True).reshape(pairs, rows, 2 * HALF)
    scale = 1.0 / math.sqrt(3 * SITES * 2 * pairs)
    share = (jnp.sum(parts.astype(jnp.float32), axis=0) * scale).astype(jnp.bfloat16)

    slices = lax.axis_size(("zl", "zh"))
    copies = jnp.broadcast_to(share[None], (slices, rows, 2 * HALF))
    gathered = lax.all_to_all(copies, ("zl", "zh"), 0, 0, tiled=True)
    sent = spread(lax.axis_index("zl")[None], source_list, gathered)
    arrived = lax.all_to_all(sent, ("core", "y", "x"), 0, 0, tiled=True)

    space_count = lax.axis_size(SPACE)
    blocks = perambulator[0].reshape(-1, 2 * NV, NV)
    value = trace(arrived, blocks, space_count)
    values = lax.all_to_all(value, SPACE, 0, 0, tiled=True)[:, :2].reshape(pairs, 2, 2)
    per_slot = jnp.sum(values, axis=1) / (NS * NV)
    one_hot = (source_list[:, None] == jnp.arange(source_list.shape[0])[None]).astype(jnp.float32)
    correlator = jnp.sum(per_slot[:, :, None] * one_hot[:, None, :], axis=0)

    own_rows = NV // space_count
    mine = lax.dynamic_index_in_dim(arrived.reshape(2, pairs, 2, rows, 2, HALF)[:, :, 0], pair_index, 1, keepdims=False)
    mine = lax.dynamic_slice_in_dim(mine, level * own_rows, own_rows, 1)
    elemental = jnp.transpose(mine, (1, 2, 0, 3)).reshape(1, own_rows, 2, NV)
    return elemental, correlator[:, None, :]


def solution(mesh):
    grid = Mesh(mesh.devices.reshape(8, 2, 4, 4, 2), ("zl", "core", "y", "x", "zh"))
    times = ("zl", "core")
    in_specs = (
        P(times, None, SPACE, None, None, None),
        P(times, None, None, SPACE, None, None, None),
        P(times, SPACE, None, None, None),
        P(times),
        P(),
        P(),
    )
    out_specs = (P(times, SPACE, None, None), P(None, times, None))
    return jax.shard_map(per_device, mesh=grid, in_specs=in_specs, out_specs=out_specs, check_vma=False)
```

time: 179 us -> 174 us (0.972)
  starting transfers between devices: 49.4 us -> 37.2 us
  waiting for transfers between devices: 69.2 us -> 77.9 us
    ppermute x2, waiting for transfers between devices: 15.7 us -> 28.8 us  [the longest x1 28.8 us: per_device(): crossed = lax.ppermute(plane, ('core', 'zh'), [(1, 0), (2, 3)])]
    ppermute x1, starting transfers between devices: 14.3 us -> 1.91 us  [per_device(): other = lax.ppermute(left, 'core', [(0, 1), (1, 0)])]
    all_to_all x2, waiting for transfers between devices: 32.2 us -> 26.6 us  [the longest x1 14.7 us: per_device(): gathered = lax.all_to_all(copies, ('zl', 'zh'), 0, 0, tiled=True)]
    pallas_call x1, Pallas kernels: 8.27 us -> 5.48 us  [trace(): pl.pallas_call(trace_kernel, out_shape=jax.ShapeDtypeStruct((copies, 128)...]
    ppermute x3, waiting for transfers between devices: 3.6 us -> 6.37 us  [moved(): lax.ppermute(value, XY, [(i, (i + distance) % pairs) for i in range(pairs)])]
    ppermute x1, waiting for transfers between devices: 2.1 us -> 0.01 us  [per_device(): other = lax.ppermute(left, 'core', [(0, 1), (1, 0)])]
    pallas_call x2 -> x3, Pallas kernels: 5.58 us -> 7.64 us  [the longest x1 2.97 us: both_pair(): pl.pallas_call(both_kernel, out_shape=jax.ShapeDtypeStruct((NV, 2 * HALF)...]
  transfers between devices with their start and end apart: 9 -> 9, of which waited for: 6 -> 6; matrix products, arithmetic and copies ran while one was open for 3% -> 3% of each run, Pallas kernels for 0% -> 2%
where the time goes in v2:
time: 174 us; the launch traced here: 173 us
  waiting for transfers between devices  77.9 us (45%)
  starting transfers between devices  37.2 us (21%)
  Pallas kernels  27.2 us (16%)
  blocking collectives  15.2 us (9%)
  local copies, waits for them, and re-layouts  7.29 us (4%)
  between operations  4.09 us (2%)
  other arithmetic  3.89 us (2%)
    ppermute x1, waiting for transfers between devices, per_device(): crossed = lax.ppermute(plane, ('core', 'zh'), [(1, 0), (2, 3)])  28.8 us
    all_to_all x1, waiting for transfers between devices, per_device(): lax.all_to_all(value, SPACE, 0, 0, tiled=True)[:, :2].reshape(pairs, 2, 2)  16.2 us
    all_to_all x1, blocking collectives, per_device(): lax.all_to_all(partial_value, XY, 0, 0, tiled=True)  15.2 us
    all_to_all x1, waiting for transfers between devices, per_device(): gathered = lax.all_to_all(copies, ('zl', 'zh'), 0, 0, tiled=True)  14.7 us
    pallas_call x1, Pallas kernels, smear(): pl.pallas_call(smear_kernel, out_shape=(jax.ShapeDtypeStruct((12, HALF, 2...  14.1 us
    ppermute x3, starting transfers between devices, moved(): lax.ppermute(value, XY, [(i, (i + distance) % pairs) for i in range(pairs)])  13.2 us
    all_to_all x1, waiting for transfers between devices, per_device(): arrived = lax.all_to_all(sent, ('core', 'y', 'x'), 0, 0, tiled=True)  11.9 us
    all_to_all x1, starting transfers between devices, per_device(): gathered = lax.all_to_all(copies, ('zl', 'zh'), 0, 0, tiled=True)  11.7 us
  transfers between devices with their start and end apart: 9, of which 6 were waited for; matrix products, arithmetic and copies ran while one was open for 3% of the time, Pallas kernels for 2%

profile of v2, /device:TPU:32, one launch (start us, length us, event | category | flops | bytes accessed | tf_op | source)
XLA Modules:
  0.0 172.7 jit_solution(6744125794193976678)
XLA Ops:
  0.6 1.0 copy.36
  3.2 1.3 collective-permute-start
  4.6 28.8 %collective-permute-done = bf16[2,832,128]{2,1,0:T(8,128)(2,1)S(1)} collective-permute-done((bf16[2,832,128]{2,1,0:T(8,128)(2,1)S(1)}, bf16[2,832,128]{2,1,0:T(8,128)(2,1)S(1)}, u32[]{:S(2)}, u32[]{:S(2)}) %collective-permute-start) | collective-permute-done | bytes 426016 | tf_op jit(solution)/shard_map/ppermute | solution.py:330
  33.5 1.3 collective-permute-start.1
  37.3 1.2 fusion.9
  39.3 3.4 %collective-permute-start.2 = (bf16[2,832,128]{2,1,0:T(8,128)(2,1)S(1)}, bf16[2,832,128]{2,1,0:T(8,128)(2,1)S(1)}, u32[]{:S(2)}, u32[]{:S(2)}) collective-permute-start(bf16[2,832,128]{2,1,0:T(8,128)(2,1)S(1)} %maximum_select_fusion.mid_ref), channel_id=1, source_target_pairs={{0,2},{2,4},{4,6},{6,8},{8,10},{10,12},{12,14},{14,16},{16,18},{18... | collective-permute-start | bytes 1277960 | tf_op jit(solution)/shard_map/ppermute | solution.py:342
  42.7 5.8 %collective-permute-start.3 = (bf16[2,832,128]{2,1,0:T(8,128)(2,1)S(1)}, bf16[2,832,128]{2,1,0:T(8,128)(2,1)S(1)}, u32[]{:S(2)}, u32[]{:S(2)}) collective-permute-start(bf16[2,832,128]{2,1,0:T(8,128)(2,1)S(1)} %maximum_select_fusion.mid_ref), channel_id=1, source_target_pairs={{0,30},{2,0},{4,2},{6,4},{8,6},{10,8},{12,10},{14,12},{16,14},{18,... | collective-permute-start | bytes 1277960 | tf_op jit(solution)/shard_map/ppermute | solution.py:342
  49.0 4.1 %collective-permute-start.4 = (bf16[768,128]{1,0:T(8,128)(2,1)S(1)}, bf16[768,128]{1,0:T(8,128)(2,1)S(1)}, u32[]{:S(2)}, u32[]{:S(2)}) collective-permute-start(bf16[768,128]{1,0:T(8,128)(2,1)S(1)} %slice_bitcast_fusion), channel_id=1, source_target_pairs={{0,28},{2,30},{4,0},{6,2},{8,4},{10,6},{12,8},{14,10},{16,12},{18,... | collective-permute-start | bytes 589832 | tf_op jit(solution)/shard_map/ppermute | solution.py:342
  54.5 3.9 %collective-permute-done.4.far_ref = bf16[768,128]{1,0:T(8,128)(2,1)S(1)} collective-permute-done((bf16[768,128]{1,0:T(8,128)(2,1)S(1)}, bf16[768,128]{1,0:T(8,128)(2,1)S(1)}, u32[]{:S(2)}, u32[]{:S(2)}) %collective-permute-start.4) | collective-permute-done | bytes 196640 | tf_op jit(solution)/shard_map/ppermute | solution.py:342
  58.4 2.4 %collective-permute-done.3.high_ref = bf16[2,832,128]{2,1,0:T(8,128)(2,1)S(1)} collective-permute-done((bf16[2,832,128]{2,1,0:T(8,128)(2,1)S(1)}, bf16[2,832,128]{2,1,0:T(8,128)(2,1)S(1)}, u32[]{:S(2)}, u32[]{:S(2)}) %collective-permute-start.3) | collective-permute-done | bytes 426016 | tf_op jit(solution)/shard_map/ppermute | solution.py:342
  61.6 14.1 %smear.1 = (bf16[12,128,256]{2,1,0:T(8,128)(2,1)}, bf16[12,256,256]{2,1,0:T(8,128)(2,1)}) custom-call(s32[1]{0:T(128)} %bitcast.6.pick_ref, f32[8,128]{1,0:T(8,128)} %bitcast.42, bf16[2,832,128]{2,1,0:T(8,128)(2,1)} %copy-done.4, bf16[2,832,128]{2,1,0:T(8,128)(2,1)} %copy-done.1, bf16[2,832,128]{2,1,0:T(8,128)(2,1)} %copy-done.5, bf16[768,128]{1,0:T(8,128)(2,1)} %copy-done.6), custom_call_target="tpu_custom_call" | custom-call | tf_op jit(solution)/shard_map/smear/pallas_call | solution.py:177
  75.7 1.9 %collective-permute-start.5 = (bf16[12,128,256]{2,1,0:T(8,128)(2,1)}, bf16[12,128,256]{2,1,0:T(8,128)(2,1)S(1)}, u32[]{:S(2)}, u32[]{:S(2)}) collective-permute-start(bf16[12,128,256]{2,1,0:T(8,128)(2,1)} %get-tuple-element.4.left_ref), channel_id=1, source_target_pairs={{0,32},{32,0},{1,33},{33,1},{2,34},{34,2},{3,35},{35,3},{4,36},{36... | collective-permute-start | bytes 2359304 | tf_op jit(solution)/shard_map/ppermute | solution.py:350
  77.6 2.9 %own_pair.1.own_ref = bf16[128,256]{1,0:T(8,128)(2,1)} custom-call(bf16[12,128,256]{2,1,0:T(8,128)(2,1)} %get-tuple-element.4.left_ref, bf16[12,256,256]{2,1,0:T(8,128)(2,1)} %get-tuple-element.5.right_ref), custom_call_target="tpu_custom_call" | custom-call | flops 201326592 | bytes 3145728 | tf_op jit(solution)/shard_map/own_pair/pallas_call | solution.py:208
  80.5 0.9 copy-done.2
  81.4 3.0 %both_pair.1 = bf16[256,256]{1,0:T(8,128)(2,1)} custom-call(s32[1]{0:T(128)} %bitcast.1.core_ref, bf16[128,256]{1,0:T(8,128)(2,1)} %own_pair.1.own_ref, bf16[12,128,256]{2,1,0:T(8,128)(2,1)} %copy-done.2, bf16[12,256,256]{2,1,0:T(8,128)(2,1)} %get-tuple-element.5.right_ref), custom_call_target="tpu_custom_call" | custom-call | tf_op jit(solution)/shard_map/both_pair/pallas_call | solution.py:225
  84.4 15.2 %all_to_all.31 = bf16[16,16,256]{2,1,0:T(8,128)(2,1)S(1)} all-to-all(bf16[16,16,256]{2,1,0:T(8,128)(2,1)} %bitcast.37), channel_id=1, replica_groups=mesh['zl'=8,'core'=2,'y'=4,'x'=4,'zh'=2] {'y','x'}, dimensions={0} | all-to-all | bytes 262144 | tf_op jit(solution)/shard_map/all_to_all | solution.py:353
  100.3 11.7 %all-to-all-start.1 = ((bf16[16,16,256]{2,1,0:T(8,128)(2,1)}), bf16[16,16,256]{2,1,0:T(8,128)(2,1)S(1)}, u32[]{:S(2)}, u32[]{:S(2)}) async-start(bf16[16,16,256]{2,1,0:T(8,128)(2,1)} %broadcast_in_dim.16), calls=%async_computation.1 | async-start | bytes 262144 | tf_op jit(solution)/shard_map/all_to_all | solution.py:359
  112.0 14.7 %all-to-all-done.1.gathered_ref = bf16[16,16,256]{2,1,0:T(8,128)(2,1)S(1)} async-done(((bf16[16,16,256]{2,1,0:T(8,128)(2,1)}), bf16[16,16,256]{2,1,0:T(8,128)(2,1)S(1)}, u32[]{:S(2)}, u32[]{:S(2)}) %all-to-all-start.1) | async-done | bytes 131104 | tf_op jit(solution)/shard_map/all_to_all | solution.py:359
  127.4 1.8 %spread.1 = bf16[32,2,16,256]{3,2,1,0:T(8,128)(2,1)} custom-call(s32[1]{0:T(128)} %bitcast.level_ref, s32[16]{0:T(128)} %source_ref.1, bf16[16,16,256]{2,1,0:T(8,128)(2,1)} %copy-done.3), custom_call_target="tpu_custom_call" | custom-call | tf_op jit(solution)/shard_map/spread/pallas_call | solution.py:245
  129.1 3.9 %all-to-all-start.2 = ((bf16[32,2,16,256]{3,2,1,0:T(8,128)(2,1)}), bf16[32,2,16,256]{3,2,1,0:T(8,128)(2,1)S(1)}, u32[]{:S(2)}, u32[]{:S(2)}) async-start(bf16[32,2,16,256]{3,2,1,0:T(8,128)(2,1)} %spread.1), calls=%async_computation.2 | async-start | bytes 1048576 | tf_op jit(solution)/shard_map/all_to_all | solution.py:361
  133.1 11.9 %all-to-all-done.2.arrived_ref = bf16[32,2,16,256]{3,2,1,0:T(8,128)(2,1)S(1)} async-done(((bf16[32,2,16,256]{3,2,1,0:T(8,128)(2,1)}), bf16[32,2,16,256]{3,2,1,0:T(8,128)(2,1)S(1)}, u32[]{:S(2)}, u32[]{:S(2)}) %all-to-all-start.2) | async-done | bytes 524320 | tf_op jit(solution)/shard_map/all_to_all | solution.py:361
  145.8 5.5 %trace.1 = f32[32,128]{1,0:T(8,128)} custom-call(bf16[32,2,16,256]{3,2,1,0:T(8,128)(2,1)} %copy-done, bf16[8,512,256]{2,1,0:T(8,128)(2,1)} %bitcast.36), custom_call_target="tpu_custom_call" | custom-call | tf_op jit(solution)/shard_map/trace/pallas_call | solution.py:292
  151.3 3.8 %all-to-all-start.3 = ((f32[32,1,128]{2,1,0:T(1,128)}), f32[32,1,128]{2,1,0:T(1,128)S(1)}, u32[]{:S(2)}, u32[]{:S(2)}) async-start(f32[32,1,128]{2,1,0:T(1,128)} %bitcast.39), calls=%async_computation.3 | async-start | bytes 32768 | tf_op jit(solution)/shard_map/all_to_all | solution.py:366
  155.8 16.2 %all-to-all-done.3 = f32[32,1,128]{2,1,0:T(1,128)S(1)} async-done(((f32[32,1,128]{2,1,0:T(1,128)}), f32[32,1,128]{2,1,0:T(1,128)S(1)}, u32[]{:S(2)}, u32[]{:S(2)}) %all-to-all-start.3) | async-done | bytes 16416 | tf_op jit(solution)/shard_map/all_to_all | solution.py:366
  (50 shorter events, 8.1 us)
Async XLA Ops:
  0.6 34.2 %copy-start.8 = (s32[3]{0:T(128)S(1)}, s32[3]{0:T(128)}, u32[]{:S(2)}) copy-start(s32[3]{0:T(128)} %param.10) | copy-start | bytes 40
  3.2 30.1 %collective-permute-start = (bf16[2,832,128]{2,1,0:T(8,128)(2,1)S(1)}, bf16[2,832,128]{2,1,0:T(8,128)(2,1)S(1)}, u32[]{:S(2)}, u32[]{:S(2)}) collective-permute-start(bf16[2,832,128]{2,1,0:T(8,128)(2,1)S(1)} %pad_maximum_fusion), channel_id=1, source_target_pairs={{1,0},{32,33},{3,2},{34,35},{5,4},{36,37},{7,6},{38,39},{9,8},{40,... | collective-permute-start | bytes 1277960 | tf_op jit(solution)/shard_map/ppermute | solution.py:330
  33.5 5.7 %collective-permute-start.1 = (bf16[2,832,128]{2,1,0:T(8,128)(2,1)S(1)}, bf16[2,832,128]{2,1,0:T(8,128)(2,1)S(1)}, u32[]{:S(2)}, u32[]{:S(2)}) collective-permute-start(bf16[2,832,128]{2,1,0:T(8,128)(2,1)S(1)} %pad_maximum_fusion.1), channel_id=1, source_target_pairs={{0,32},{33,1},{2,34},{35,3},{4,36},{37,5},{6,38},{39,7},{8,40},{41... | collective-permute-start | bytes 1277960 | tf_op jit(solution)/shard_map/ppermute | solution.py:338
  39.3 21.6 %copy-start.1 = (bf16[2,832,128]{2,1,0:T(8,128)(2,1)}, bf16[2,832,128]{2,1,0:T(8,128)(2,1)S(1)}, u32[]{:S(2)}) copy-start(bf16[2,832,128]{2,1,0:T(8,128)(2,1)S(1)} %maximum_select_fusion.mid_ref) | copy-start | bytes 1277956
  39.3 19.1 %collective-permute-start.2 = (bf16[2,832,128]{2,1,0:T(8,128)(2,1)S(1)}, bf16[2,832,128]{2,1,0:T(8,128)(2,1)S(1)}, u32[]{:S(2)}, u32[]{:S(2)}) collective-permute-start(bf16[2,832,128]{2,1,0:T(8,128)(2,1)S(1)} %maximum_select_fusion.mid_ref), channel_id=1, source_target_pairs={{0,2},{2,4},{4,6},{6,8},{8,10},{10,12},{12,14},{14,16},{16,18},{18... | collective-permute-start | bytes 1277960 | tf_op jit(solution)/shard_map/ppermute | solution.py:342
  42.7 18.1 %collective-permute-start.3 = (bf16[2,832,128]{2,1,0:T(8,128)(2,1)S(1)}, bf16[2,832,128]{2,1,0:T(8,128)(2,1)S(1)}, u32[]{:S(2)}, u32[]{:S(2)}) collective-permute-start(bf16[2,832,128]{2,1,0:T(8,128)(2,1)S(1)} %maximum_select_fusion.mid_ref), channel_id=1, source_target_pairs={{0,30},{2,0},{4,2},{6,4},{8,6},{10,8},{12,10},{14,12},{16,14},{18,... | collective-permute-start | bytes 1277960 | tf_op jit(solution)/shard_map/ppermute | solution.py:342
  49.0 9.4 %collective-permute-start.4 = (bf16[768,128]{1,0:T(8,128)(2,1)S(1)}, bf16[768,128]{1,0:T(8,128)(2,1)S(1)}, u32[]{:S(2)}, u32[]{:S(2)}) collective-permute-start(bf16[768,128]{1,0:T(8,128)(2,1)S(1)} %slice_bitcast_fusion), channel_id=1, source_target_pairs={{0,28},{2,30},{4,0},{6,2},{8,4},{10,6},{12,8},{14,10},{16,12},{18,... | collective-permute-start | bytes 589832 | tf_op jit(solution)/shard_map/ppermute | solution.py:342
  58.4 2.4 %copy-start.6 = (bf16[768,128]{1,0:T(8,128)(2,1)}, bf16[768,128]{1,0:T(8,128)(2,1)S(1)}, u32[]{:S(2)}) copy-start(bf16[768,128]{1,0:T(8,128)(2,1)S(1)} %collective-permute-done.4.far_ref) | copy-start | bytes 589828
  58.4 2.4 %copy-start.4 = (bf16[2,832,128]{2,1,0:T(8,128)(2,1)}, bf16[2,832,128]{2,1,0:T(8,128)(2,1)S(1)}, u32[]{:S(2)}) copy-start(bf16[2,832,128]{2,1,0:T(8,128)(2,1)S(1)} %collective-permute-done.2.low_ref) | copy-start | bytes 1277956
  60.8 0.8 copy-start.5
  75.7 4.8 %collective-permute-start.5 = (bf16[12,128,256]{2,1,0:T(8,128)(2,1)}, bf16[12,128,256]{2,1,0:T(8,128)(2,1)S(1)}, u32[]{:S(2)}, u32[]{:S(2)}) collective-permute-start(bf16[12,128,256]{2,1,0:T(8,128)(2,1)} %get-tuple-element.4.left_ref), channel_id=1, source_target_pairs={{0,32},{32,0},{1,33},{33,1},{2,34},{34,2},{3,35},{35,3},{4,36},{36... | collective-permute-start | bytes 2359304 | tf_op jit(solution)/shard_map/ppermute | solution.py:350
  80.5 0.9 copy-start.2
  81.4 51.6 %copy-start.7 = (s32[16]{0:T(128)S(1)}, s32[16]{0:T(128)}, u32[]{:S(2)}) copy-start(s32[16]{0:T(128)} %source_ref.1) | copy-start | bytes 196
  100.3 26.5 %all-to-all-start.1 = ((bf16[16,16,256]{2,1,0:T(8,128)(2,1)}), bf16[16,16,256]{2,1,0:T(8,128)(2,1)S(1)}, u32[]{:S(2)}, u32[]{:S(2)}) async-start(bf16[16,16,256]{2,1,0:T(8,128)(2,1)} %broadcast_in_dim.16), calls=%async_computation.1 | async-start | bytes 262144 | tf_op jit(solution)/shard_map/all_to_all | solution.py:359
  126.7 0.6 copy-start.3
  129.1 15.9 %all-to-all-start.2 = ((bf16[32,2,16,256]{3,2,1,0:T(8,128)(2,1)}), bf16[32,2,16,256]{3,2,1,0:T(8,128)(2,1)S(1)}, u32[]{:S(2)}, u32[]{:S(2)}) async-start(bf16[32,2,16,256]{3,2,1,0:T(8,128)(2,1)} %spread.1), calls=%async_computation.2 | async-start | bytes 1048576 | tf_op jit(solution)/shard_map/all_to_all | solution.py:361
  145.0 0.8 copy-start
  151.3 20.7 %all-to-all-start.3 = ((f32[32,1,128]{2,1,0:T(1,128)}), f32[32,1,128]{2,1,0:T(1,128)S(1)}, u32[]{:S(2)}, u32[]{:S(2)}) async-start(f32[32,1,128]{2,1,0:T(1,128)} %bitcast.39), calls=%async_computation.3 | async-start | bytes 32768 | tf_op jit(solution)/shard_map/all_to_all | solution.py:366

commit v3 on v2

--- a/solution.py
+++ b/solution.py
@@ -6,6 +6,7 @@
 from jax.experimental import pallas as pl
 from jax.experimental.pallas import tpu as pltpu
 from jax.sharding import Mesh, PartitionSpec as P
+
 
 NV = 256
 NS = 4
@@ -42,22 +43,40 @@
     return jnp.where(first, roll_lanes(value, 1 - SX), roll_lanes(value, 1))
 
 
-def smear_kernel(pick_ref, phase_ref, low_ref, mid_ref, high_ref, far_ref, left_ref, right_ref, link_ref, one_ref, two_ref):
+def smear_kernel(pick_ref, level_ref, phase_ref, *refs):
+    low, mid, high, far = refs[0:2], refs[2:4], refs[4:6], refs[6:8]
+    left_ref, right_ref, link_ref, field_ref, one_ref, two_ref = refs[8:]
+
+    def load(even):
+        for index, group in enumerate((low, mid, high)):
+            for parity in range(2):
+                source = group[parity if even else 1 - parity]
+                field_ref[index * 2 + parity] = source[pl.ds(0, VROWS), :].astype(jnp.float32)
+                link_ref[index * 2 + parity, pl.ds(0, LROWS), :] = source[pl.ds(VROWS, LROWS), :].astype(jnp.float32)
+        field_ref[6] = far[0 if even else 1][...].astype(jnp.float32)
+
+    @pl.when(level_ref[0] == 0)
+    def _():
+        load(True)
+
+    @pl.when(level_ref[0] != 0)
+    def _():
+        load(False)
+
     site = lax.broadcasted_iota(jnp.int32, (18, SITES), 1) % SX
-    for plane in range(6):
-        source = (low_ref, mid_ref, high_ref)[plane // 2]
-        block = source[plane % 2, pl.ds(VROWS, LROWS), :].astype(jnp.float32)
-        rows = [block[index : index + 1] for index in range(54)]
-        if plane:
-            behind = behind_x(block[0:18], site == 0)
-            below = roll_lanes(block[18:36], SX)
-            rows += [behind[index : index + 1] for index in range(18)]
-            rows += [below[index : index + 1] for index in range(18)]
-        for index in range(36 if plane == 0 else 0, len(rows)):
-            link_ref[plane, index] = jnp.broadcast_to(rows[index], (CHUNK, SITES)).astype(jnp.bfloat16)
+    for plane in range(1, 6):
+        link_ref[plane, pl.ds(64, 18), :] = behind_x(link_ref[plane, pl.ds(0, 18), :], site == 0)
+        link_ref[plane, pl.ds(88, 18), :] = roll_lanes(link_ref[plane, pl.ds(18, 18), :], SX)
 
     def link(plane, base):
-        return lambda part, row, column: link_ref[plane, base + part * 9 + row * 3 + column]
+        def get(part, row, column):
+            line = link_ref[plane, pl.ds(base + part * 9 + row * 3 + column, 1), :]
+            return jnp.broadcast_to(line, (CHUNK, SITES))
+
+        return get
+
+    def packed(matrix):
+        return lambda *at: matrix(*at).astype(jnp.bfloat16)
 
     def apply(total, matrix, field, adjoint):
         for row in range(3):
@@ -82,19 +101,21 @@
         zero = jnp.zeros((CHUNK, SITES), kind)
         return [[zero for _ in range(3)] for _ in range(2)]
 
+    def narrow(field):
+        return each(field, lambda v: v.astype(jnp.bfloat16))
+
     def sweep(plane, here, above, below):
         total = zeros(jnp.bfloat16)
-        apply(total, link(plane, 0), each(here, lambda v: ahead_x(v, last)), False)
-        apply(total, link(plane, 54), each(here, lambda v: behind_x(v, first)), True)
-        apply(total, link(plane, 18), each(here, lambda v: roll_lanes(v, -SX)), False)
-        apply(total, link(plane, 72), each(here, lambda v: roll_lanes(v, SX)), True)
-        apply(total, link(plane, 36), above, False)
-        apply(total, link(plane - 1, 36), below, True)
+        middle = narrow(here)
+        apply(total, packed(link(plane, 0)), each(middle, lambda v: ahead_x(v, last)), False)
+        apply(total, packed(link(plane, 64)), each(middle, lambda v: behind_x(v, first)), True)
+        apply(total, packed(link(plane, 18)), each(middle, lambda v: roll_lanes(v, -SX)), False)
+        apply(total, packed(link(plane, 88)), each(middle, lambda v: roll_lanes(v, SX)), True)
+        apply(total, packed(link(plane, 36)), narrow(above), False)
+        apply(total, packed(link(plane - 1, 36)), narrow(below), True)
 
         def joined(part, colour):
-            middle = here[part][colour].astype(jnp.float32)
-            change = total[part][colour].astype(jnp.float32) - 6.0 * middle
-            return (middle + KAPPA * change).astype(jnp.bfloat16)
+            return (1.0 - 6.0 * KAPPA) * here[part][colour] + KAPPA * total[part][colour].astype(jnp.float32)
 
         return [[joined(part, colour) for colour in range(3)] for part in range(2)]
 
@@ -102,14 +123,10 @@
         start = pl.multiple_of(chunk * CHUNK, CHUNK)
 
         def start_field(plane):
-            def get(part, colour):
-                rows = pl.ds((part * 3 + colour) * HALF + start, CHUNK)
-                if plane == 6:
-                    return far_ref[rows, :]
-                source = (low_ref, mid_ref, high_ref)[plane // 2]
-                return source[plane % 2, rows, :]
-
-            return [[get(part, colour) for colour in range(3)] for part in range(2)]
+            return [
+                [field_ref[plane, pl.ds((part * 3 + colour) * HALF + start, CHUNK), :] for colour in range(3)]
+                for part in range(2)
+            ]
 
         def stored(ref, plane):
             return [[ref[plane, part * 3 + colour] for colour in range(3)] for part in range(2)]
@@ -126,8 +143,7 @@
                     two_ref[plane, part * 3 + colour] = result[part][colour]
         for side in range(2):
             plane = side + 2
-            here = each(stored(two_ref, plane), lambda v: v.astype(jnp.float32))
-            above = each(stored(two_ref, plane + 1), lambda v: v.astype(jnp.float32))
+            here, above = stored(two_ref, plane), stored(two_ref, plane + 1)
             incoming = [
                 [
                     jnp.where(
@@ -140,8 +156,7 @@
                 for part in range(2)
             ]
             moved = zeros(jnp.float32)
-            chosen = link(plane, pick * 18)
-            apply(moved, lambda *at: chosen(*at).astype(jnp.float32), incoming, False)
+            apply(moved, link(plane, pick * 18), incoming, False)
 
             def row_of(index):
                 return phase_ref[pl.ds(side * 4 + index, 1), :]
@@ -173,62 +188,54 @@
     lax.fori_loop(0, HALF // CHUNK, step, 0)
 
 
-def smear(pick, phase, low, mid, high, far):
+def room(megabytes):
+    return pltpu.CompilerParams(vmem_limit_bytes=megabytes * 2**20)
+
+
+def smear(pick, level, phase, *planes):
     return pl.pallas_call(
         smear_kernel,
         out_shape=(
             jax.ShapeDtypeStruct((12, HALF, 2 * SITES), jnp.bfloat16),
             jax.ShapeDtypeStruct((12, 2 * HALF, 2 * SITES), jnp.bfloat16),
         ),
-        in_specs=[scalar(), whole(), whole(), whole(), whole(), whole()],
+        in_specs=[scalar(), scalar()] + [whole()] * (1 + len(planes)),
         out_specs=(whole(), whole()),
         scratch_shapes=[
-            pltpu.VMEM((6, 90, CHUNK, SITES), jnp.bfloat16),
-            pltpu.VMEM((6, 6, CHUNK, SITES), jnp.bfloat16),
-            pltpu.VMEM((5, 6, CHUNK, SITES), jnp.bfloat16),
+            pltpu.VMEM((6, 112, SITES), jnp.float32),
+            pltpu.VMEM((7, VROWS, SITES), jnp.float32),
+            pltpu.VMEM((6, 6, CHUNK, SITES), jnp.float32),
+            pltpu.VMEM((5, 6, CHUNK, SITES), jnp.float32),
         ],
+        compiler_params=room(14),
         name="smear",
-    )(pick, phase, low, mid, high, far)
-
-
-def product(left_ref, right_ref):
-    total = jnp.zeros((HALF, 2 * HALF), jnp.float32)
-    for index in range(12):
-        total += lax.dot_general(
-            left_ref[index], right_ref[index], (((1,), (1,)), ((), ())), preferred_element_type=jnp.float32
-        )
-    return total.astype(jnp.bfloat16)
-
-
-def own_kernel(left_ref, right_ref, out_ref):
-    out_ref[...] = product(left_ref, right_ref)
-
-
-def own_pair(left, right):
+    )(pick, level, phase, *planes)
+
+
+def pair_kernel(core_ref, own_ref, other_ref, right_ref, out_ref):
+    core = core_ref[0]
+
+    def product(ref):
+        total = jnp.zeros((HALF, 2 * HALF), jnp.float32)
+        for index in range(12):
+            total += lax.dot_general(
+                ref[index], right_ref[index], (((1,), (1,)), ((), ())), preferred_element_type=jnp.float32
+            )
+        return total.astype(jnp.bfloat16)
+
+    out_ref[pl.ds(pl.multiple_of(core * HALF, HALF), HALF), :] = product(own_ref)
+    out_ref[pl.ds(pl.multiple_of((1 - core) * HALF, HALF), HALF), :] = product(other_ref)
+
+
+def pair(core, own, other, right):
     return pl.pallas_call(
-        own_kernel,
-        out_shape=jax.ShapeDtypeStruct((HALF, 2 * HALF), jnp.bfloat16),
-        in_specs=[whole(), whole()],
-        out_specs=whole(),
-        cost_estimate=pl.CostEstimate(flops=2 * 12 * HALF * 2 * HALF * 2 * SITES, bytes_accessed=3 * 2**20, transcendentals=0),
-        name="own_pair",
-    )(left, right)
-
-
-def both_kernel(core_ref, own_ref, left_ref, right_ref, out_ref):
-    core = core_ref[0]
-    out_ref[pl.ds(pl.multiple_of(core * HALF, HALF), HALF), :] = own_ref[...]
-    out_ref[pl.ds(pl.multiple_of((1 - core) * HALF, HALF), HALF), :] = product(left_ref, right_ref)
-
-
-def both_pair(core, own, left, right):
-    return pl.pallas_call(
-        both_kernel,
+        pair_kernel,
         out_shape=jax.ShapeDtypeStruct((NV, 2 * HALF), jnp.bfloat16),
         in_specs=[scalar(), whole(), whole(), whole()],
         out_specs=whole(),
-        name="both_pair",
-    )(core, own, left, right)
+        compiler_params=room(8),
+        name="pair",
+    )(core, own, other, right)
 
 
 def spread_kernel(level_ref, source_ref, gathered_ref, out_ref):
@@ -247,6 +254,7 @@
         out_shape=jax.ShapeDtypeStruct((2 * source_list.shape[0], 2, rows, 2 * HALF), jnp.bfloat16),
         in_specs=[scalar(), scalar(), whole()],
         out_specs=whole(),
+        compiler_params=room(4),
         name="spread",
     )(level, source_list, gathered)
 
@@ -295,6 +303,7 @@
         in_specs=[whole(), whole()],
         out_specs=whole(),
         scratch_shapes=[pltpu.VMEM((2 * NV, 2 * NV), jnp.bfloat16), pltpu.VMEM((NV, 2 * NV), jnp.bfloat16)],
+        compiler_params=room(12),
         name="trace",
     )(arrived, blocks)
 
@@ -322,33 +331,40 @@
     pairs = lax.axis_size(XY)
     rows = NV // pairs
 
-    halves = jnp.swapaxes(vectors[0, :, 0].reshape(6, 2, HALF, SITES), 0, 1).reshape(2, VROWS, SITES)
-    link_rows = gauge_links[0, :, :, 0].reshape(54, SITES).astype(jnp.bfloat16)
+    links = gauge_links[0, :, :, 0].reshape(54, SITES).astype(jnp.bfloat16)
     pick_row = jnp.broadcast_to(directions[0].astype(jnp.bfloat16), (LROWS - 54, SITES))
-    tail = jnp.concatenate([link_rows, pick_row], axis=0)
-    plane = jnp.concatenate([halves, jnp.broadcast_to(tail[None], (2, LROWS, SITES))], axis=1)
-    crossed = lax.ppermute(plane, ("core", "zh"), [(1, 0), (2, 3)])
-    even = level == 0
-
-    def both_planes(index):
-        near = lax.dynamic_index_in_dim(plane, index, 0, keepdims=False)
-        away = lax.dynamic_index_in_dim(crossed, index, 0, keepdims=False)
-        return jnp.stack([jnp.where(even, near, away), jnp.where(even, away, near)])
-
-    taken = lax.ppermute(both_planes(1 - core), ("core", "zh"), [(0, 2), (3, 1)])
-    mid = jnp.where(core == level, both_planes(core), taken)
-
-    def moved(value, distance):
-        return lax.ppermute(value, XY, [(i, (i + distance) % pairs) for i in range(pairs)])
-
-    high = moved(mid, -1)
-    low = moved(mid, 1)
-    far = moved(mid[0, :VROWS], -2)
-    pick = mid[0, VROWS + 54, 0].astype(jnp.int32)
+    tail = jnp.concatenate([links, pick_row], axis=0)
+    own_vectors = vectors[0, :, 0].reshape(6, NV, SITES)
+    sites = ("core", "zh")
+    cross_vectors = lax.ppermute(own_vectors, sites, [(1, 0), (2, 3)])
+    cross_tail = lax.ppermute(tail, sites, [(1, 0), (2, 3)])
+    same = core == level
+
+    def share_out(planes, rows_of_links):
+        def half_of(index):
+            half = lax.dynamic_slice_in_dim(planes, index * HALF, HALF, 1).reshape(VROWS, SITES)
+            return jnp.concatenate([half, rows_of_links], axis=0)
+
+        taken = lax.ppermute(half_of(1 - core), sites, [(0, 2), (3, 1)])
+        return jnp.where(same, half_of(core), taken)
+
+    def moved(value, distance, levels):
+        route = [(i * 2 + z, (i + distance) % pairs * 2 + z) for i in range(pairs) for z in levels]
+        return lax.ppermute(value, SPACE, route)
+
+    def around(plane, far_levels):
+        low, high = moved(plane, 1, (0, 1)), moved(plane, -1, (0, 1))
+        return low, plane, high, moved(plane[:VROWS], -2, far_levels)
+
+    own = around(share_out(own_vectors, tail), (0,))
+    own, cross_vectors, cross_tail = lax.optimization_barrier((own, cross_vectors, cross_tail))
+    other = around(share_out(cross_vectors, cross_tail), (1,))
+    pick = own[1][VROWS + 54, 0].astype(jnp.int32)
     phase = phases(momentum, pick, pair_index, 2 * pairs)
-    left, right = smear(pick[None], phase, low, mid, high, far)
-    other = lax.ppermute(left, "core", [(0, 1), (1, 0)])
-    partial_value = both_pair(core[None], own_pair(left, right), other, right)
+    planes = [plane for couple in zip(own, other) for plane in couple]
+    left, right = smear(pick[None], level[None], phase, *planes)
+    sibling = lax.ppermute(left, "core", [(0, 1), (1, 0)])
+    partial_value = pair(core[None], left, sibling, right)
 
     parts = lax.all_to_all(partial_value, XY, 0, 0, tiled=True).reshape(pairs, rows, 2 * HALF)
     scale = 1.0 / math.sqrt(3 * SITES * 2 * pairs)
@@ -387,4 +403,5 @@
         P(),
     )
     out_specs = (P(times, SPACE, None, None), P(None, times, None))
+
     return jax.shard_map(per_device, mesh=grid, in_specs=in_specs, out_specs=out_specs, check_vma=False)

time: 174 us -> 158 us (0.908)
  starting transfers between devices: 37.2 us -> 57.8 us
  waiting for transfers between devices: 77.9 us -> 59.3 us
  Pallas kernels: 27.2 us -> 13.1 us
  local copies, waits for them, and re-layouts: 7.29 us -> 4.07 us
    ppermute x6 -> x11, waiting for transfers between devices: 35.1 us -> 16.8 us  [the longest x1 11.5 us: per_device(): cross_tail = lax.ppermute(tail, sites, [(1, 0), (2, 3)])]
    ppermute x6 -> x11, starting transfers between devices: 17.7 us -> 34.7 us  [the longest x6 23.1 us: moved(): return lax.ppermute(value, SPACE, route)]
    pallas_call x1, Pallas kernels: 14.1 us -> 6.83 us  [smear(): pl.pallas_call(smear_kernel, out_shape=(jax.ShapeDtypeStruct((12, HALF, 2...]
    pallas_call x2 -> x1, Pallas kernels: 5.88 us -> 1.12 us  [pair(): pl.pallas_call(pair_kernel, out_shape=jax.ShapeDtypeStruct((NV, 2 * HALF)...]
    all_to_all x1, starting transfers between devices: 11.7 us -> 15.4 us  [per_device(): gathered = lax.all_to_all(copies, ('zl', 'zh'), 0, 0, tiled=True)]
    unnamed x22 -> x10, local copies, waits for them, and re-layouts: 3.49 us -> 0.72 us
    pallas_call x1, Pallas kernels: 5.48 us -> 3.73 us  [trace(): pl.pallas_call(trace_kernel, out_shape=jax.ShapeDtypeStruct((copies, 128)...]
  transfers between devices with their start and end apart: 9 -> 14, of which waited for: 6 -> 7; matrix products, arithmetic and copies ran while one was open for 3% -> 3% of each run, Pallas kernels for 2% -> 0%
where the time goes in v3:
time: 158 us
  waiting for transfers between devices  59.3 us (38%)
  starting transfers between devices  57.8 us (37%)
  blocking collectives  15.1 us (10%)
  Pallas kernels  13.1 us (8%)
  between operations  4.19 us (3%)
  local copies, waits for them, and re-layouts  4.07 us (3%)
  other arithmetic  4.03 us (3%)
    ppermute x6, starting transfers between devices, moved(): return lax.ppermute(value, SPACE, route)  23.1 us
    all_to_all x1, waiting for transfers between devices, per_device(): lax.all_to_all(value, SPACE, 0, 0, tiled=True)[:, :2].reshape(pairs, 2, 2)  16.3 us
    all_to_all x1, starting transfers between devices, per_device(): gathered = lax.all_to_all(copies, ('zl', 'zh'), 0, 0, tiled=True)  15.4 us
    all_to_all x1, blocking collectives, per_device(): lax.all_to_all(partial_value, XY, 0, 0, tiled=True)  15.1 us
    all_to_all x1, waiting for transfers between devices, per_device(): gathered = lax.all_to_all(copies, ('zl', 'zh'), 0, 0, tiled=True)  14.3 us
    all_to_all x1, waiting for transfers between devices, per_device(): arrived = lax.all_to_all(sent, ('core', 'y', 'x'), 0, 0, tiled=True)  11.9 us
    ppermute x1, waiting for transfers between devices, per_device(): cross_tail = lax.ppermute(tail, sites, [(1, 0), (2, 3)])  11.5 us
    ppermute x2, starting transfers between devices, share_out(): taken = lax.ppermute(half_of(1 - core), sites, [(0, 2), (3, 1)])  7.11 us
  transfers between devices with their start and end apart: 14, of which 7 were waited for; matrix products, arithmetic and copies ran while one was open for 3% of the time, Pallas kernels for 0%

profile of v3, /device:TPU:32, one launch (start us, length us, event | category | flops | bytes accessed | tf_op | source)
XLA Modules:
  0.0 157.6 jit_solution(10337544284546342780)
XLA Ops:
  3.5 1.8 %collective-permute-start = (bf16[832,128]{1,0:T(8,128)(2,1)S(1)}, bf16[832,128]{1,0:T(8,128)(2,1)S(1)}, u32[]{:S(2)}, u32[]{:S(2)}) collective-permute-start(bf16[832,128]{1,0:T(8,128)(2,1)S(1)} %fusion.3), channel_id=1, source_target_pairs={{0,32},{33,1},{2,34},{35,3},{4,36},{37,5},{6,38},{39,7},{8,40},{41... | collective-permute-start | bytes 638984 | tf_op jit(solution)/shard_map/ppermute | solution.py:348
  5.2 1.3 collective-permute-start.4
  6.7 3.4 %collective-permute-start.1 = (bf16[832,128]{1,0:T(8,128)(2,1)S(1)}, bf16[832,128]{1,0:T(8,128)(2,1)S(1)}, u32[]{:S(2)}, u32[]{:S(2)}) collective-permute-start(bf16[832,128]{1,0:T(8,128)(2,1)S(1)} %fusion.2.refs_2_), channel_id=1, source_target_pairs={{0,2},{1,3},{2,4},{3,5},{4,6},{5,7},{6,8},{7,9},{8,10},{9,11},{10,... | collective-permute-start | bytes 638984 | tf_op jit(solution)/shard_map/ppermute | solution.py:353
  10.2 5.8 %collective-permute-start.2 = (bf16[832,128]{1,0:T(8,128)(2,1)S(1)}, bf16[832,128]{1,0:T(8,128)(2,1)S(1)}, u32[]{:S(2)}, u32[]{:S(2)}) collective-permute-start(bf16[832,128]{1,0:T(8,128)(2,1)S(1)} %fusion.2.refs_2_), channel_id=1, source_target_pairs={{0,30},{1,31},{2,0},{3,1},{4,2},{5,3},{6,4},{7,5},{8,6},{9,7},{10,... | collective-permute-start | bytes 638984 | tf_op jit(solution)/shard_map/ppermute | solution.py:353
  15.9 4.1 %collective-permute-start.3 = (bf16[768,128]{1,0:T(8,128)(2,1)S(1)}, bf16[768,128]{1,0:T(8,128)(2,1)S(1)}, u32[]{:S(2)}, u32[]{:S(2)}) collective-permute-start(bf16[768,128]{1,0:T(8,128)(2,1)S(1)} %slice.35), channel_id=1, source_target_pairs={{0,28},{2,30},{4,0},{6,2},{8,4},{10,6},{12,8},{14,10},{16,12},{18,... | collective-permute-start | bytes 589832 | tf_op jit(solution)/shard_map/ppermute | solution.py:353
  20.0 1.3 collective-permute-start.5
  23.8 11.5 %collective-permute-done.5 = bf16[64,128]{1,0:T(8,128)(2,1)S(1)} collective-permute-done((bf16[64,128]{1,0:T(8,128)(2,1)S(1)}, bf16[64,128]{1,0:T(8,128)(2,1)S(1)}, u32[]{:S(2)}, u32[]{:S(2)}) %collective-permute-start.5) | collective-permute-done | bytes 16416 | tf_op jit(solution)/shard_map/ppermute | solution.py:340
  35.4 5.4 %collective-permute-start.6 = (bf16[832,128]{1,0:T(8,128)(2,1)S(1)}, bf16[832,128]{1,0:T(8,128)(2,1)S(1)}, u32[]{:S(2)}, u32[]{:S(2)}) collective-permute-start(bf16[832,128]{1,0:T(8,128)(2,1)S(1)} %pad_maximum_fusion.2), channel_id=1, source_target_pairs={{0,32},{33,1},{2,34},{35,3},{4,36},{37,5},{6,38},{39,7},{8,40},{41... | collective-permute-start | bytes 638984 | tf_op jit(solution)/shard_map/ppermute | solution.py:348
  40.7 1.2 fusion.11
  43.9 3.4 %collective-permute-start.7 = (bf16[832,128]{1,0:T(8,128)(2,1)S(1)}, bf16[832,128]{1,0:T(8,128)(2,1)S(1)}, u32[]{:S(2)}, u32[]{:S(2)}) collective-permute-start(bf16[832,128]{1,0:T(8,128)(2,1)S(1)} %fusion.refs_3_), channel_id=1, source_target_pairs={{0,2},{1,3},{2,4},{3,5},{4,6},{5,7},{6,8},{7,9},{8,10},{9,11},{10,... | collective-permute-start | bytes 638984 | tf_op jit(solution)/shard_map/ppermute | solution.py:353
  47.3 5.8 %collective-permute-start.8 = (bf16[832,128]{1,0:T(8,128)(2,1)S(1)}, bf16[832,128]{1,0:T(8,128)(2,1)S(1)}, u32[]{:S(2)}, u32[]{:S(2)}) collective-permute-start(bf16[832,128]{1,0:T(8,128)(2,1)S(1)} %fusion.refs_3_), channel_id=1, source_target_pairs={{0,30},{1,31},{2,0},{3,1},{4,2},{5,3},{6,4},{7,5},{8,6},{9,7},{10,... | collective-permute-start | bytes 638984 | tf_op jit(solution)/shard_map/ppermute | solution.py:353
  53.9 1.9 %collective-permute-done.7.refs_1_ = bf16[832,128]{1,0:T(8,128)(2,1)S(1)} collective-permute-done((bf16[832,128]{1,0:T(8,128)(2,1)S(1)}, bf16[832,128]{1,0:T(8,128)(2,1)S(1)}, u32[]{:S(2)}, u32[]{:S(2)}) %collective-permute-start.7) | collective-permute-done | bytes 213024 | tf_op jit(solution)/shard_map/ppermute | solution.py:353
  57.0 6.8 %smear.1 = (bf16[12,128,256]{2,1,0:T(8,128)(2,1)S(1)}, bf16[12,256,256]{2,1,0:T(8,128)(2,1)S(1)}) custom-call(s32[1]{0:T(128)} %bitcast.6.pick_ref, s32[1]{0:T(128)} %bitcast.7.level_ref, f32[8,128]{1,0:T(8,128)S(1)} %bitcast.36, bf16[832,128]{1,0:T(8,128)(2,1)S(1)} %collective-permute-done.1.refs_0_, bf16[832,128]{1,0:T(8,128)(2,1)S(1)} %collective-permute-done.7.refs_1_, ...), custom_call_target="tpu_custom_call" | custom-call | tf_op jit(solution)/shard_map/smear/pallas_call | solution.py:196
  63.8 1.9 %collective-permute-start.10 = (bf16[12,128,256]{2,1,0:T(8,128)(2,1)S(1)}, bf16[12,128,256]{2,1,0:T(8,128)(2,1)S(1)}, u32[]{:S(2)}, u32[]{:S(2)}) collective-permute-start(bf16[12,128,256]{2,1,0:T(8,128)(2,1)S(1)} %get-tuple-element.16.own_ref), channel_id=1, source_target_pairs={{0,32},{32,0},{1,33},{33,1},{2,34},{34,2},{3,35},{35,3},{4,36},{36... | collective-permute-start | bytes 2359304 | tf_op jit(solution)/shard_map/ppermute | solution.py:366
  65.8 2.3 %collective-permute-done.10.other_ref = bf16[12,128,256]{2,1,0:T(8,128)(2,1)S(1)} collective-permute-done((bf16[12,128,256]{2,1,0:T(8,128)(2,1)S(1)}, bf16[12,128,256]{2,1,0:T(8,128)(2,1)S(1)}, u32[]{:S(2)}, u32[]{:S(2)}) %collective-permute-start.10) | collective-permute-done | bytes 786464 | tf_op jit(solution)/shard_map/ppermute | solution.py:366
  69.1 15.1 %all_to_all.31 = bf16[16,16,256]{2,1,0:T(8,128)(2,1)S(1)} all-to-all(bf16[16,16,256]{2,1,0:T(8,128)(2,1)S(1)} %bitcast.35), channel_id=1, replica_groups=mesh['zl'=8,'core'=2,'y'=4,'x'=4,'zh'=2] {'y','x'}, dimensions={0} | all-to-all | bytes 262144 | tf_op jit(solution)/shard_map/all_to_all | solution.py:369
  85.0 15.4 %all-to-all-start.1 = ((bf16[16,16,256]{2,1,0:T(8,128)(2,1)}), bf16[16,16,256]{2,1,0:T(8,128)(2,1)S(1)}, u32[]{:S(2)}, u32[]{:S(2)}) async-start(bf16[16,16,256]{2,1,0:T(8,128)(2,1)} %broadcast_in_dim.36), calls=%async_computation.1 | async-start | bytes 262144 | tf_op jit(solution)/shard_map/all_to_all | solution.py:375
  100.4 14.3 %all-to-all-done.1.gathered_ref = bf16[16,16,256]{2,1,0:T(8,128)(2,1)S(1)} async-done(((bf16[16,16,256]{2,1,0:T(8,128)(2,1)}), bf16[16,16,256]{2,1,0:T(8,128)(2,1)S(1)}, u32[]{:S(2)}, u32[]{:S(2)}) %all-to-all-start.1) | async-done | bytes 131104 | tf_op jit(solution)/shard_map/all_to_all | solution.py:375
  114.7 1.4 spread.1
  116.1 3.9 %all-to-all-start.2 = ((bf16[32,2,16,256]{3,2,1,0:T(8,128)(2,1)}), bf16[32,2,16,256]{3,2,1,0:T(8,128)(2,1)S(1)}, u32[]{:S(2)}, u32[]{:S(2)}) async-start(bf16[32,2,16,256]{3,2,1,0:T(8,128)(2,1)} %spread.1), calls=%async_computation.2 | async-start | bytes 1048576 | tf_op jit(solution)/shard_map/all_to_all | solution.py:377
  120.1 11.9 %all-to-all-done.2.arrived_ref = bf16[32,2,16,256]{3,2,1,0:T(8,128)(2,1)S(1)} async-done(((bf16[32,2,16,256]{3,2,1,0:T(8,128)(2,1)}), bf16[32,2,16,256]{3,2,1,0:T(8,128)(2,1)S(1)}, u32[]{:S(2)}, u32[]{:S(2)}) %all-to-all-start.2) | async-done | bytes 524320 | tf_op jit(solution)/shard_map/all_to_all | solution.py:377
  132.3 3.7 %trace.1 = f32[32,128]{1,0:T(8,128)} custom-call(bf16[32,2,16,256]{3,2,1,0:T(8,128)(2,1)S(1)} %all-to-all-done.2.arrived_ref, bf16[8,512,256]{2,1,0:T(8,128)(2,1)S(1)} %bitcast.34), custom_call_target="tpu_custom_call" | custom-call | tf_op jit(solution)/shard_map/trace/pallas_call | solution.py:300
  136.0 3.8 %all-to-all-start.3 = ((f32[32,1,128]{2,1,0:T(1,128)}), f32[32,1,128]{2,1,0:T(1,128)S(1)}, u32[]{:S(2)}, u32[]{:S(2)}) async-start(f32[32,1,128]{2,1,0:T(1,128)} %bitcast.21), calls=%async_computation.3 | async-start | bytes 32768 | tf_op jit(solution)/shard_map/all_to_all | solution.py:382
  140.5 16.3 %all-to-all-done.3 = f32[32,1,128]{2,1,0:T(1,128)S(1)} async-done(((f32[32,1,128]{2,1,0:T(1,128)}), f32[32,1,128]{2,1,0:T(1,128)S(1)}, u32[]{:S(2)}, u32[]{:S(2)}) %all-to-all-start.3) | async-done | bytes 16416 | tf_op jit(solution)/shard_map/all_to_all | solution.py:382
  (50 shorter events, 9.9 us)
Async XLA Ops:
  0.6 20.7 %copy-start.2 = (s32[3]{0:T(128)S(1)}, s32[3]{0:T(128)}, u32[]{:S(2)}) copy-start(s32[3]{0:T(128)} %param.10) | copy-start | bytes 40
  3.5 3.1 %collective-permute-start = (bf16[832,128]{1,0:T(8,128)(2,1)S(1)}, bf16[832,128]{1,0:T(8,128)(2,1)S(1)}, u32[]{:S(2)}, u32[]{:S(2)}) collective-permute-start(bf16[832,128]{1,0:T(8,128)(2,1)S(1)} %fusion.3), channel_id=1, source_target_pairs={{0,32},{33,1},{2,34},{35,3},{4,36},{37,5},{6,38},{39,7},{8,40},{41... | collective-permute-start | bytes 638984 | tf_op jit(solution)/shard_map/ppermute | solution.py:348
  5.2 30.1 %collective-permute-start.4 = (bf16[6,256,128]{2,1,0:T(8,128)(2,1)}, bf16[6,256,128]{2,1,0:T(8,128)(2,1)S(1)}, u32[]{:S(2)}, u32[]{:S(2)}) collective-permute-start(bf16[6,256,128]{2,1,0:T(8,128)(2,1)} %bitcast.42), channel_id=1, source_target_pairs={{1,0},{32,33},{3,2},{34,35},{5,4},{36,37},{7,6},{38,39},{9,8},{40,... | collective-permute-start | bytes 1179656 | tf_op jit(solution)/shard_map/ppermute | solution.py:339
  6.7 28.6 %collective-permute-start.1 = (bf16[832,128]{1,0:T(8,128)(2,1)S(1)}, bf16[832,128]{1,0:T(8,128)(2,1)S(1)}, u32[]{:S(2)}, u32[]{:S(2)}) collective-permute-start(bf16[832,128]{1,0:T(8,128)(2,1)S(1)} %fusion.2.refs_2_), channel_id=1, source_target_pairs={{0,2},{1,3},{2,4},{3,5},{4,6},{5,7},{6,8},{7,9},{8,10},{9,11},{10,... | collective-permute-start | bytes 638984 | tf_op jit(solution)/shard_map/ppermute | solution.py:353
  10.2 25.2 %collective-permute-start.2 = (bf16[832,128]{1,0:T(8,128)(2,1)S(1)}, bf16[832,128]{1,0:T(8,128)(2,1)S(1)}, u32[]{:S(2)}, u32[]{:S(2)}) collective-permute-start(bf16[832,128]{1,0:T(8,128)(2,1)S(1)} %fusion.2.refs_2_), channel_id=1, source_target_pairs={{0,30},{1,31},{2,0},{3,1},{4,2},{5,3},{6,4},{7,5},{8,6},{9,7},{10,... | collective-permute-start | bytes 638984 | tf_op jit(solution)/shard_map/ppermute | solution.py:353
  15.9 19.4 %collective-permute-start.3 = (bf16[768,128]{1,0:T(8,128)(2,1)S(1)}, bf16[768,128]{1,0:T(8,128)(2,1)S(1)}, u32[]{:S(2)}, u32[]{:S(2)}) collective-permute-start(bf16[768,128]{1,0:T(8,128)(2,1)S(1)} %slice.35), channel_id=1, source_target_pairs={{0,28},{2,30},{4,0},{6,2},{8,4},{10,6},{12,8},{14,10},{16,12},{18,... | collective-permute-start | bytes 589832 | tf_op jit(solution)/shard_map/ppermute | solution.py:353
  20.0 15.3 %collective-permute-start.5 = (bf16[64,128]{1,0:T(8,128)(2,1)S(1)}, bf16[64,128]{1,0:T(8,128)(2,1)S(1)}, u32[]{:S(2)}, u32[]{:S(2)}) collective-permute-start(bf16[64,128]{1,0:T(8,128)(2,1)S(1)} %concatenate.19), channel_id=1, source_target_pairs={{1,0},{32,33},{3,2},{34,35},{5,4},{36,37},{7,6},{38,39},{9,8},{40,... | collective-permute-start | bytes 49160 | tf_op jit(solution)/shard_map/ppermute | solution.py:340
  35.4 8.4 %collective-permute-start.6 = (bf16[832,128]{1,0:T(8,128)(2,1)S(1)}, bf16[832,128]{1,0:T(8,128)(2,1)S(1)}, u32[]{:S(2)}, u32[]{:S(2)}) collective-permute-start(bf16[832,128]{1,0:T(8,128)(2,1)S(1)} %pad_maximum_fusion.2), channel_id=1, source_target_pairs={{0,32},{33,1},{2,34},{35,3},{4,36},{37,5},{6,38},{39,7},{8,40},{41... | collective-permute-start | bytes 638984 | tf_op jit(solution)/shard_map/ppermute | solution.py:348
  43.9 11.9 %collective-permute-start.7 = (bf16[832,128]{1,0:T(8,128)(2,1)S(1)}, bf16[832,128]{1,0:T(8,128)(2,1)S(1)}, u32[]{:S(2)}, u32[]{:S(2)}) collective-permute-start(bf16[832,128]{1,0:T(8,128)(2,1)S(1)} %fusion.refs_3_), channel_id=1, source_target_pairs={{0,2},{1,3},{2,4},{3,5},{4,6},{5,7},{6,8},{7,9},{8,10},{9,11},{10,... | collective-permute-start | bytes 638984 | tf_op jit(solution)/shard_map/ppermute | solution.py:353
  47.3 9.7 %collective-permute-start.8 = (bf16[832,128]{1,0:T(8,128)(2,1)S(1)}, bf16[832,128]{1,0:T(8,128)(2,1)S(1)}, u32[]{:S(2)}, u32[]{:S(2)}) collective-permute-start(bf16[832,128]{1,0:T(8,128)(2,1)S(1)} %fusion.refs_3_), channel_id=1, source_target_pairs={{0,30},{1,31},{2,0},{3,1},{4,2},{5,3},{6,4},{7,5},{8,6},{9,7},{10,... | collective-permute-start | bytes 638984 | tf_op jit(solution)/shard_map/ppermute | solution.py:353
  53.1 0.8 collective-permute-start.9
  63.8 50.9 %copy-start.1 = (s32[16]{0:T(128)S(1)}, s32[16]{0:T(128)}, u32[]{:S(2)}) copy-start(s32[16]{0:T(128)} %source_ref.1) | copy-start | bytes 196
  63.8 4.2 %collective-permute-start.10 = (bf16[12,128,256]{2,1,0:T(8,128)(2,1)S(1)}, bf16[12,128,256]{2,1,0:T(8,128)(2,1)S(1)}, u32[]{:S(2)}, u32[]{:S(2)}) collective-permute-start(bf16[12,128,256]{2,1,0:T(8,128)(2,1)S(1)} %get-tuple-element.16.own_ref), channel_id=1, source_target_pairs={{0,32},{32,0},{1,33},{33,1},{2,34},{34,2},{3,35},{35,3},{4,36},{36... | collective-permute-start | bytes 2359304 | tf_op jit(solution)/shard_map/ppermute | solution.py:366
  69.1 63.2 %copy-start = (bf16[1,8,2,256,256]{4,3,2,1,0:T(8,128)(2,1)S(1)}, bf16[1,8,2,256,256]{4,3,2,1,0:T(8,128)(2,1)}, u32[]{:S(2)}) copy-start(bf16[1,8,2,256,256]{4,3,2,1,0:T(8,128)(2,1)} %param.8) | copy-start | bytes 6291460
  85.0 29.8 %all-to-all-start.1 = ((bf16[16,16,256]{2,1,0:T(8,128)(2,1)}), bf16[16,16,256]{2,1,0:T(8,128)(2,1)S(1)}, u32[]{:S(2)}, u32[]{:S(2)}) async-start(bf16[16,16,256]{2,1,0:T(8,128)(2,1)} %broadcast_in_dim.36), calls=%async_computation.1 | async-start | bytes 262144 | tf_op jit(solution)/shard_map/all_to_all | solution.py:375
  116.1 15.9 %all-to-all-start.2 = ((bf16[32,2,16,256]{3,2,1,0:T(8,128)(2,1)}), bf16[32,2,16,256]{3,2,1,0:T(8,128)(2,1)S(1)}, u32[]{:S(2)}, u32[]{:S(2)}) async-start(bf16[32,2,16,256]{3,2,1,0:T(8,128)(2,1)} %spread.1), calls=%async_computation.2 | async-start | bytes 1048576 | tf_op jit(solution)/shard_map/all_to_all | solution.py:377
  136.0 20.8 %all-to-all-start.3 = ((f32[32,1,128]{2,1,0:T(1,128)}), f32[32,1,128]{2,1,0:T(1,128)S(1)}, u32[]{:S(2)}, u32[]{:S(2)}) async-start(f32[32,1,128]{2,1,0:T(1,128)} %bitcast.21), calls=%async_computation.3 | async-start | bytes 32768 | tf_op jit(solution)/shard_map/all_to_all | solution.py:382

commit v4 on v3

--- a/solution.py
+++ b/solution.py
@@ -334,19 +334,17 @@
     links = gauge_links[0, :, :, 0].reshape(54, SITES).astype(jnp.bfloat16)
     pick_row = jnp.broadcast_to(directions[0].astype(jnp.bfloat16), (LROWS - 54, SITES))
     tail = jnp.concatenate([links, pick_row], axis=0)
-    own_vectors = vectors[0, :, 0].reshape(6, NV, SITES)
+    planes_here = vectors[0, :, 0].reshape(6, NV, SITES)
     sites = ("core", "zh")
-    cross_vectors = lax.ppermute(own_vectors, sites, [(1, 0), (2, 3)])
-    cross_tail = lax.ppermute(tail, sites, [(1, 0), (2, 3)])
     same = core == level
 
-    def share_out(planes, rows_of_links):
-        def half_of(index):
-            half = lax.dynamic_slice_in_dim(planes, index * HALF, HALF, 1).reshape(VROWS, SITES)
-            return jnp.concatenate([half, rows_of_links], axis=0)
-
-        taken = lax.ppermute(half_of(1 - core), sites, [(0, 2), (3, 1)])
-        return jnp.where(same, half_of(core), taken)
+    def half_of(index):
+        half = lax.dynamic_slice_in_dim(planes_here, index * HALF, HALF, 1).reshape(VROWS, SITES)
+        return jnp.concatenate([half, tail], axis=0)
+
+    first_half, second_half = lax.optimization_barrier((half_of(core), half_of(1 - core)))
+    cross_same = lax.ppermute(first_half, sites, [(1, 0), (2, 3)])
+    cross_sibling = lax.ppermute(second_half, sites, [(1, 2), (2, 1)])
 
     def moved(value, distance, levels):
         route = [(i * 2 + z, (i + distance) % pairs * 2 + z) for i in range(pairs) for z in levels]
@@ -356,9 +354,10 @@
         low, high = moved(plane, 1, (0, 1)), moved(plane, -1, (0, 1))
         return low, plane, high, moved(plane[:VROWS], -2, far_levels)
 
-    own = around(share_out(own_vectors, tail), (0,))
-    own, cross_vectors, cross_tail = lax.optimization_barrier((own, cross_vectors, cross_tail))
-    other = around(share_out(cross_vectors, cross_tail), (1,))
+    taken = lax.ppermute(second_half, sites, [(0, 2), (3, 1)])
+    own = around(jnp.where(same, first_half, taken), (0,))
+    own, cross_same, cross_sibling = lax.optimization_barrier((own, cross_same, cross_sibling))
+    other = around(jnp.where(same, cross_same, cross_sibling), (1,))
     pick = own[1][VROWS + 54, 0].astype(jnp.int32)
     phase = phases(momentum, pick, pair_index, 2 * pairs)
     planes = [plane for couple in zip(own, other) for plane in couple]

time: 158 us -> 151 us (0.956)
  starting transfers between devices: 57.8 us -> 50.5 us
    ppermute x4 -> x3, starting transfers between devices: 9.69 us -> 3.72 us  [the longest x1 1.75 us: per_device(): taken = lax.ppermute(second_half, sites, [(0, 2), (3, 1)])]
    all_to_all x1, starting transfers between devices: 15.4 us -> 12.3 us  [per_device(): gathered = lax.all_to_all(copies, ('zl', 'zh'), 0, 0, tiled=True)]
    ppermute x1, starting transfers between devices: 1.92 us -> 3.67 us  [per_device(): sibling = lax.ppermute(left, 'core', [(0, 1), (1, 0)])]
    ppermute x4 -> x3, waiting for transfers between devices: 11.5 us -> 12.6 us  [the longest x1 12.6 us: per_device(): cross_same = lax.ppermute(first_half, sites, [(1, 0), (2, 3)])]
  transfers between devices with their start and end apart: 14 -> 13, of which waited for: 7 -> 7; matrix products, arithmetic and copies ran while one was open for 3% -> 3% of each run, Pallas kernels for 0% -> 0%
where the time goes in v4:
time: 151 us; the launch traced here: 150 us
  waiting for transfers between devices  58.9 us (39%)
  starting transfers between devices  50.5 us (33%)
  blocking collectives  15.1 us (10%)
  Pallas kernels  13.1 us (9%)
  other arithmetic  4.46 us (3%)
  between operations  4.11 us (3%)
  local copies, waits for them, and re-layouts  4.07 us (3%)
    ppermute x6, starting transfers between devices, moved(): return lax.ppermute(value, SPACE, route)  23.1 us
    all_to_all x1, waiting for transfers between devices, per_device(): lax.all_to_all(value, SPACE, 0, 0, tiled=True)[:, :2].reshape(pairs, 2, 2)  16.2 us
    all_to_all x1, blocking collectives, per_device(): lax.all_to_all(partial_value, XY, 0, 0, tiled=True)  15.1 us
    all_to_all x1, waiting for transfers between devices, per_device(): gathered = lax.all_to_all(copies, ('zl', 'zh'), 0, 0, tiled=True)  14.3 us
    ppermute x1, waiting for transfers between devices, per_device(): cross_same = lax.ppermute(first_half, sites, [(1, 0), (2, 3)])  12.6 us
    all_to_all x1, starting transfers between devices, per_device(): gathered = lax.all_to_all(copies, ('zl', 'zh'), 0, 0, tiled=True)  12.3 us
    all_to_all x1, waiting for transfers between devices, per_device(): arrived = lax.all_to_all(sent, ('core', 'y', 'x'), 0, 0, tiled=True)  11.9 us
    pallas_call x1, Pallas kernels, smear(): pl.pallas_call(smear_kernel, out_shape=(jax.ShapeDtypeStruct((12, HALF, 2...  6.83 us
  transfers between devices with their start and end apart: 13, of which 7 were waited for; matrix products, arithmetic and copies ran while one was open for 3% of the time, Pallas kernels for 0%

profile of v4, /device:TPU:32, one launch (start us, length us, event | category | flops | bytes accessed | tf_op | source)
XLA Modules:
  0.0 150.1 jit_solution(4433012882193873116)
XLA Ops:
  2.2 1.0 constant_dynamic-slice_fusion.1
  3.5 1.8 %collective-permute-start = (bf16[832,128]{1,0:T(8,128)(2,1)S(1)}, bf16[832,128]{1,0:T(8,128)(2,1)S(1)}, u32[]{:S(2)}, u32[]{:S(2)}) collective-permute-start(bf16[832,128]{1,0:T(8,128)(2,1)S(1)} %get-tuple-element.13), channel_id=1, source_target_pairs={{0,32},{33,1},{2,34},{35,3},{4,36},{37,5},{6,38},{39,7},{8,40},{41... | collective-permute-start | bytes 638984 | tf_op jit(solution)/shard_map/ppermute | solution.py:357
  5.9 1.3 collective-permute-start.4
  10.4 3.4 %collective-permute-start.1 = (bf16[832,128]{1,0:T(8,128)(2,1)S(1)}, bf16[832,128]{1,0:T(8,128)(2,1)S(1)}, u32[]{:S(2)}, u32[]{:S(2)}) collective-permute-start(bf16[832,128]{1,0:T(8,128)(2,1)S(1)} %broadcast_select_fusion.1.refs_2_), channel_id=1, source_target_pairs={{0,2},{1,3},{2,4},{3,5},{4,6},{5,7},{6,8},{7,9},{8,10},{9,11},{10,... | collective-permute-start | bytes 638984 | tf_op jit(solution)/shard_map/ppermute | solution.py:351
  13.8 5.8 %collective-permute-start.2 = (bf16[832,128]{1,0:T(8,128)(2,1)S(1)}, bf16[832,128]{1,0:T(8,128)(2,1)S(1)}, u32[]{:S(2)}, u32[]{:S(2)}) collective-permute-start(bf16[832,128]{1,0:T(8,128)(2,1)S(1)} %broadcast_select_fusion.1.refs_2_), channel_id=1, source_target_pairs={{0,30},{1,31},{2,0},{3,1},{4,2},{5,3},{6,4},{7,5},{8,6},{9,7},{10,... | collective-permute-start | bytes 638984 | tf_op jit(solution)/shard_map/ppermute | solution.py:351
  19.6 4.1 %collective-permute-start.3 = (bf16[768,128]{1,0:T(8,128)(2,1)S(1)}, bf16[768,128]{1,0:T(8,128)(2,1)S(1)}, u32[]{:S(2)}, u32[]{:S(2)}) collective-permute-start(bf16[768,128]{1,0:T(8,128)(2,1)S(1)} %slice.35), channel_id=1, source_target_pairs={{0,28},{2,30},{4,0},{6,2},{8,4},{10,6},{12,8},{14,10},{16,12},{18,... | collective-permute-start | bytes 589832 | tf_op jit(solution)/shard_map/ppermute | solution.py:351
  23.7 1.2 fusion.9
  25.5 12.6 %collective-permute-done.4 = bf16[832,128]{1,0:T(8,128)(2,1)S(1)} collective-permute-done((bf16[832,128]{1,0:T(8,128)(2,1)S(1)}, bf16[832,128]{1,0:T(8,128)(2,1)S(1)}, u32[]{:S(2)}, u32[]{:S(2)}) %collective-permute-start.4) | collective-permute-done | bytes 213024 | tf_op jit(solution)/shard_map/ppermute | solution.py:346
  38.2 3.4 %collective-permute-start.6 = (bf16[832,128]{1,0:T(8,128)(2,1)S(1)}, bf16[832,128]{1,0:T(8,128)(2,1)S(1)}, u32[]{:S(2)}, u32[]{:S(2)}) collective-permute-start(bf16[832,128]{1,0:T(8,128)(2,1)S(1)} %broadcast_select_fusion.refs_3_), channel_id=1, source_target_pairs={{0,2},{1,3},{2,4},{3,5},{4,6},{5,7},{6,8},{7,9},{8,10},{9,11},{10,... | collective-permute-start | bytes 638984 | tf_op jit(solution)/shard_map/ppermute | solution.py:351
  41.6 5.8 %collective-permute-start.7 = (bf16[832,128]{1,0:T(8,128)(2,1)S(1)}, bf16[832,128]{1,0:T(8,128)(2,1)S(1)}, u32[]{:S(2)}, u32[]{:S(2)}) collective-permute-start(bf16[832,128]{1,0:T(8,128)(2,1)S(1)} %broadcast_select_fusion.refs_3_), channel_id=1, source_target_pairs={{0,30},{1,31},{2,0},{3,1},{4,2},{5,3},{6,4},{7,5},{8,6},{9,7},{10,... | collective-permute-start | bytes 638984 | tf_op jit(solution)/shard_map/ppermute | solution.py:351
  49.6 1.7 %collective-permute-done.7.refs_5_ = bf16[832,128]{1,0:T(8,128)(2,1)S(1)} collective-permute-done((bf16[832,128]{1,0:T(8,128)(2,1)S(1)}, bf16[832,128]{1,0:T(8,128)(2,1)S(1)}, u32[]{:S(2)}, u32[]{:S(2)}) %collective-permute-start.7) | collective-permute-done | bytes 213024 | tf_op jit(solution)/shard_map/ppermute | solution.py:351
  51.4 6.8 %smear.1 = (bf16[12,128,256]{2,1,0:T(8,128)(2,1)S(1)}, bf16[12,256,256]{2,1,0:T(8,128)(2,1)S(1)}) custom-call(s32[1]{0:T(128)} %bitcast.6.pick_ref, s32[1]{0:T(128)} %bitcast.7.level_ref, f32[8,128]{1,0:T(8,128)S(1)} %bitcast.34, bf16[832,128]{1,0:T(8,128)(2,1)S(1)} %collective-permute-done.1.refs_0_, bf16[832,128]{1,0:T(8,128)(2,1)S(1)} %collective-permute-done.6.refs_1_, ...), custom_call_target="tpu_custom_call" | custom-call | tf_op jit(solution)/shard_map/smear/pallas_call | solution.py:196
  58.2 3.7 %collective-permute-start.9 = (bf16[12,128,256]{2,1,0:T(8,128)(2,1)S(1)}, bf16[12,128,256]{2,1,0:T(8,128)(2,1)S(1)}, u32[]{:S(2)}, u32[]{:S(2)}) collective-permute-start(bf16[12,128,256]{2,1,0:T(8,128)(2,1)S(1)} %get-tuple-element.20.own_ref), channel_id=1, source_target_pairs={{0,32},{32,0},{1,33},{33,1},{2,34},{34,2},{3,35},{35,3},{4,36},{36... | collective-permute-start | bytes 2359304 | tf_op jit(solution)/shard_map/ppermute | solution.py:365
  61.9 1.9 %collective-permute-done.9.other_ref = bf16[12,128,256]{2,1,0:T(8,128)(2,1)S(1)} collective-permute-done((bf16[12,128,256]{2,1,0:T(8,128)(2,1)S(1)}, bf16[12,128,256]{2,1,0:T(8,128)(2,1)S(1)}, u32[]{:S(2)}, u32[]{:S(2)}) %collective-permute-start.9) | collective-permute-done | bytes 786464 | tf_op jit(solution)/shard_map/ppermute | solution.py:365
  63.8 1.1 pair.1
  64.9 15.1 %all_to_all.31 = bf16[16,16,256]{2,1,0:T(8,128)(2,1)S(1)} all-to-all(bf16[16,16,256]{2,1,0:T(8,128)(2,1)S(1)} %bitcast.33), channel_id=1, replica_groups=mesh['zl'=8,'core'=2,'y'=4,'x'=4,'zh'=2] {'y','x'}, dimensions={0} | all-to-all | bytes 262144 | tf_op jit(solution)/shard_map/all_to_all | solution.py:368
  80.7 12.3 %all-to-all-start.1 = ((bf16[16,16,256]{2,1,0:T(8,128)(2,1)}), bf16[16,16,256]{2,1,0:T(8,128)(2,1)S(1)}, u32[]{:S(2)}, u32[]{:S(2)}) async-start(bf16[16,16,256]{2,1,0:T(8,128)(2,1)} %broadcast_in_dim.36), calls=%async_computation.1 | async-start | bytes 262144 | tf_op jit(solution)/shard_map/all_to_all | solution.py:374
  93.0 14.3 %all-to-all-done.1.gathered_ref = bf16[16,16,256]{2,1,0:T(8,128)(2,1)S(1)} async-done(((bf16[16,16,256]{2,1,0:T(8,128)(2,1)}), bf16[16,16,256]{2,1,0:T(8,128)(2,1)S(1)}, u32[]{:S(2)}, u32[]{:S(2)}) %all-to-all-start.1) | async-done | bytes 131104 | tf_op jit(solution)/shard_map/all_to_all | solution.py:374
  107.4 1.4 spread.1
  108.8 3.9 %all-to-all-start.2 = ((bf16[32,2,16,256]{3,2,1,0:T(8,128)(2,1)}), bf16[32,2,16,256]{3,2,1,0:T(8,128)(2,1)S(1)}, u32[]{:S(2)}, u32[]{:S(2)}) async-start(bf16[32,2,16,256]{3,2,1,0:T(8,128)(2,1)} %spread.1), calls=%async_computation.2 | async-start | bytes 1048576 | tf_op jit(solution)/shard_map/all_to_all | solution.py:376
  112.7 11.9 %all-to-all-done.2.arrived_ref = bf16[32,2,16,256]{3,2,1,0:T(8,128)(2,1)S(1)} async-done(((bf16[32,2,16,256]{3,2,1,0:T(8,128)(2,1)}), bf16[32,2,16,256]{3,2,1,0:T(8,128)(2,1)S(1)}, u32[]{:S(2)}, u32[]{:S(2)}) %all-to-all-start.2) | async-done | bytes 524320 | tf_op jit(solution)/shard_map/all_to_all | solution.py:376
  125.0 3.7 %trace.1 = f32[32,128]{1,0:T(8,128)} custom-call(bf16[32,2,16,256]{3,2,1,0:T(8,128)(2,1)S(1)} %all-to-all-done.2.arrived_ref, bf16[8,512,256]{2,1,0:T(8,128)(2,1)S(1)} %bitcast.32), custom_call_target="tpu_custom_call" | custom-call | tf_op jit(solution)/shard_map/trace/pallas_call | solution.py:300
  128.7 3.8 %all-to-all-start.3 = ((f32[32,1,128]{2,1,0:T(1,128)}), f32[32,1,128]{2,1,0:T(1,128)S(1)}, u32[]{:S(2)}, u32[]{:S(2)}) async-start(f32[32,1,128]{2,1,0:T(1,128)} %bitcast.19), calls=%async_computation.3 | async-start | bytes 32768 | tf_op jit(solution)/shard_map/all_to_all | solution.py:381
  133.2 16.2 %all-to-all-done.3 = f32[32,1,128]{2,1,0:T(1,128)S(1)} async-done(((f32[32,1,128]{2,1,0:T(1,128)}), f32[32,1,128]{2,1,0:T(1,128)S(1)}, u32[]{:S(2)}, u32[]{:S(2)}) %all-to-all-start.3) | async-done | bytes 16416 | tf_op jit(solution)/shard_map/all_to_all | solution.py:381
  (43 shorter events, 7.8 us)
Async XLA Ops:
  3.5 6.9 %collective-permute-start = (bf16[832,128]{1,0:T(8,128)(2,1)S(1)}, bf16[832,128]{1,0:T(8,128)(2,1)S(1)}, u32[]{:S(2)}, u32[]{:S(2)}) collective-permute-start(bf16[832,128]{1,0:T(8,128)(2,1)S(1)} %get-tuple-element.13), channel_id=1, source_target_pairs={{0,32},{33,1},{2,34},{35,3},{4,36},{37,5},{6,38},{39,7},{8,40},{41... | collective-permute-start | bytes 638984 | tf_op jit(solution)/shard_map/ppermute | solution.py:357
  5.2 32.9 %collective-permute-start.5 = (bf16[832,128]{1,0:T(8,128)(2,1)S(1)}, bf16[832,128]{1,0:T(8,128)(2,1)S(1)}, u32[]{:S(2)}, u32[]{:S(2)}) collective-permute-start(bf16[832,128]{1,0:T(8,128)(2,1)S(1)} %get-tuple-element.13), channel_id=1, source_target_pairs={{1,32},{32,1},{3,34},{34,3},{5,36},{36,5},{7,38},{38,7},{9,40},{40... | collective-permute-start | bytes 638984 | tf_op jit(solution)/shard_map/ppermute | solution.py:347
  5.9 32.2 %collective-permute-start.4 = (bf16[832,128]{1,0:T(8,128)(2,1)S(1)}, bf16[832,128]{1,0:T(8,128)(2,1)S(1)}, u32[]{:S(2)}, u32[]{:S(2)}) collective-permute-start(bf16[832,128]{1,0:T(8,128)(2,1)S(1)} %get-tuple-element.12), channel_id=1, source_target_pairs={{1,0},{32,33},{3,2},{34,35},{5,4},{36,37},{7,6},{38,39},{9,8},{40,... | collective-permute-start | bytes 638984 | tf_op jit(solution)/shard_map/ppermute | solution.py:346
  10.4 27.7 %collective-permute-start.1 = (bf16[832,128]{1,0:T(8,128)(2,1)S(1)}, bf16[832,128]{1,0:T(8,128)(2,1)S(1)}, u32[]{:S(2)}, u32[]{:S(2)}) collective-permute-start(bf16[832,128]{1,0:T(8,128)(2,1)S(1)} %broadcast_select_fusion.1.refs_2_), channel_id=1, source_target_pairs={{0,2},{1,3},{2,4},{3,5},{4,6},{5,7},{6,8},{7,9},{8,10},{9,11},{10,... | collective-permute-start | bytes 638984 | tf_op jit(solution)/shard_map/ppermute | solution.py:351
  13.8 24.3 %collective-permute-start.2 = (bf16[832,128]{1,0:T(8,128)(2,1)S(1)}, bf16[832,128]{1,0:T(8,128)(2,1)S(1)}, u32[]{:S(2)}, u32[]{:S(2)}) collective-permute-start(bf16[832,128]{1,0:T(8,128)(2,1)S(1)} %broadcast_select_fusion.1.refs_2_), channel_id=1, source_target_pairs={{0,30},{1,31},{2,0},{3,1},{4,2},{5,3},{6,4},{7,5},{8,6},{9,7},{10,... | collective-permute-start | bytes 638984 | tf_op jit(solution)/shard_map/ppermute | solution.py:351
  19.6 18.5 %collective-permute-start.3 = (bf16[768,128]{1,0:T(8,128)(2,1)S(1)}, bf16[768,128]{1,0:T(8,128)(2,1)S(1)}, u32[]{:S(2)}, u32[]{:S(2)}) collective-permute-start(bf16[768,128]{1,0:T(8,128)(2,1)S(1)} %slice.35), channel_id=1, source_target_pairs={{0,28},{2,30},{4,0},{6,2},{8,4},{10,6},{12,8},{14,10},{16,12},{18,... | collective-permute-start | bytes 589832 | tf_op jit(solution)/shard_map/ppermute | solution.py:351
  38.2 11.4 %collective-permute-start.6 = (bf16[832,128]{1,0:T(8,128)(2,1)S(1)}, bf16[832,128]{1,0:T(8,128)(2,1)S(1)}, u32[]{:S(2)}, u32[]{:S(2)}) collective-permute-start(bf16[832,128]{1,0:T(8,128)(2,1)S(1)} %broadcast_select_fusion.refs_3_), channel_id=1, source_target_pairs={{0,2},{1,3},{2,4},{3,5},{4,6},{5,7},{6,8},{7,9},{8,10},{9,11},{10,... | collective-permute-start | bytes 638984 | tf_op jit(solution)/shard_map/ppermute | solution.py:351
  41.6 9.7 %collective-permute-start.7 = (bf16[832,128]{1,0:T(8,128)(2,1)S(1)}, bf16[832,128]{1,0:T(8,128)(2,1)S(1)}, u32[]{:S(2)}, u32[]{:S(2)}) collective-permute-start(bf16[832,128]{1,0:T(8,128)(2,1)S(1)} %broadcast_select_fusion.refs_3_), channel_id=1, source_target_pairs={{0,30},{1,31},{2,0},{3,1},{4,2},{5,3},{6,4},{7,5},{8,6},{9,7},{10,... | collective-permute-start | bytes 638984 | tf_op jit(solution)/shard_map/ppermute | solution.py:351
  47.4 2.0 %collective-permute-start.8 = (bf16[768,128]{1,0:T(8,128)(2,1)S(1)}, bf16[768,128]{1,0:T(8,128)(2,1)S(1)}, u32[]{:S(2)}, u32[]{:S(2)}) collective-permute-start(bf16[768,128]{1,0:T(8,128)(2,1)S(1)} %slice.36), channel_id=1, source_target_pairs={{1,29},{3,31},{5,1},{7,3},{9,5},{11,7},{13,9},{15,11},{17,13},{19,... | collective-permute-start | bytes 589832 | tf_op jit(solution)/shard_map/ppermute | solution.py:351
  58.2 49.2 %copy-start.1 = (s32[16]{0:T(128)S(1)}, s32[16]{0:T(128)}, u32[]{:S(2)}) copy-start(s32[16]{0:T(128)} %source_ref.1) | copy-start | bytes 196
  58.2 5.6 %collective-permute-start.9 = (bf16[12,128,256]{2,1,0:T(8,128)(2,1)S(1)}, bf16[12,128,256]{2,1,0:T(8,128)(2,1)S(1)}, u32[]{:S(2)}, u32[]{:S(2)}) collective-permute-start(bf16[12,128,256]{2,1,0:T(8,128)(2,1)S(1)} %get-tuple-element.20.own_ref), channel_id=1, source_target_pairs={{0,32},{32,0},{1,33},{33,1},{2,34},{34,2},{3,35},{35,3},{4,36},{36... | collective-permute-start | bytes 2359304 | tf_op jit(solution)/shard_map/ppermute | solution.py:365
  64.9 60.0 %copy-start = (bf16[1,8,2,256,256]{4,3,2,1,0:T(8,128)(2,1)S(1)}, bf16[1,8,2,256,256]{4,3,2,1,0:T(8,128)(2,1)}, u32[]{:S(2)}) copy-start(bf16[1,8,2,256,256]{4,3,2,1,0:T(8,128)(2,1)} %param.8) | copy-start | bytes 6291460
  80.7 26.6 %all-to-all-start.1 = ((bf16[16,16,256]{2,1,0:T(8,128)(2,1)}), bf16[16,16,256]{2,1,0:T(8,128)(2,1)S(1)}, u32[]{:S(2)}, u32[]{:S(2)}) async-start(bf16[16,16,256]{2,1,0:T(8,128)(2,1)} %broadcast_in_dim.36), calls=%async_computation.1 | async-start | bytes 262144 | tf_op jit(solution)/shard_map/all_to_all | solution.py:374
  108.8 15.9 %all-to-all-start.2 = ((bf16[32,2,16,256]{3,2,1,0:T(8,128)(2,1)}), bf16[32,2,16,256]{3,2,1,0:T(8,128)(2,1)S(1)}, u32[]{:S(2)}, u32[]{:S(2)}) async-start(bf16[32,2,16,256]{3,2,1,0:T(8,128)(2,1)} %spread.1), calls=%async_computation.2 | async-start | bytes 1048576 | tf_op jit(solution)/shard_map/all_to_all | solution.py:376
  128.7 20.7 %all-to-all-start.3 = ((f32[32,1,128]{2,1,0:T(1,128)}), f32[32,1,128]{2,1,0:T(1,128)S(1)}, u32[]{:S(2)}, u32[]{:S(2)}) async-start(f32[32,1,128]{2,1,0:T(1,128)} %bitcast.19), calls=%async_computation.3 | async-start | bytes 32768 | tf_op jit(solution)/shard_map/all_to_all | solution.py:381
